TPU v7x, 512 devices: a whole 4x4x16 slice. The times are simulated.
512 devices in a mesh: seq: 32 (over y, x, core), head: 16 (over z).
Axes of the slice: x: 4, y: 4, z: 16, core: 2. Of those that a mesh axis runs over, the one named last changes fastest.
Arguments:
- queries: bfloat16 [4096, 2048], P('seq', 'head'), may hold values from -6 to 6
- keys: bfloat16 [4096, 2048], P('seq', 'head'), may hold values from -6 to 6
- values: bfloat16 [4096, 4096], P('seq', 'head'), may hold values from -6 to 6
- gate_code: int32 [4096, 32], P('seq', 'head'), may hold values from 1 to 1000
- beta_code: int32 [4096, 32], P('seq', 'head'), may hold values from 1 to 255
- out_grad: bfloat16 [4096, 2048], P('seq', 'head'), may hold values from -6 to 6
- w_out: bfloat16 [4096, 2048], P('head'), may hold values from -0.09375 to 0.09375
Outputs:
- attn_out: bfloat16 [4096, 4096], P('seq', 'head')
- q_grad: float32 [4096, 2048], P('seq', 'head')
- k_grad: float32 [4096, 2048], P('seq', 'head')
- v_grad: float32 [4096, 4096], P('seq', 'head')
- weight_grad: float32 [4096, 2048], P(('head', 'seq'))
All inputs are finite; a program needn't handle non-finite values.
Results may differ from a plain program's by a relative error of at most 0.0029.
Values may be sent and summed in bfloat16 or wider, within the bound.
No kernel may reach another device: no remote copies, remote signals or barrier semaphores. Data moves between devices by JAX's collectives and lax.ppermute only.
A program may use at most 64 MiB of HBM per device.

v0:
```python
import jax
import jax.numpy as jnp
from jax import lax
from jax.sharding import PartitionSpec as P

HEAD_DIM = 128
SPAN = 64
norm_eps = 1e-06
gate_step = 1e-06
beta_steps = 256.0
highest = lax.Precision.HIGHEST


def from_behind(value, axis, steps):
    count = lax.axis_size(axis)
    initial, last = (max(0, -steps), min(count, count - steps))
    return lax.ppermute(value, axis, [(source, source + steps) for source in range(initial, last)])


def normalize(block_rows):
    return block_rows * lax.rsqrt(
        jnp.sum(block_rows * block_rows, axis=-1, keepdims=True) + norm_eps
    )


def block_masks(block):
    row_ids = lax.broadcasted_iota(jnp.int32, (block, block), 0)
    col_ids = lax.broadcasted_iota(jnp.int32, (block, block), 1)
    return (row_ids > col_ids, row_ids >= col_ids)


def span_pass(query_blocks, key_blocks, value_blocks, decay_blocks, beta_blocks, state):
    strict, inclusive = block_masks(query_blocks.shape[1])

    def span_advance(state, pieces):
        query_block, key_block, value_block, decay_log, beta_block = pieces
        log_cum = jnp.cumsum(decay_log)
        decay_cum = jnp.exp(log_cum)
        ratio = jnp.exp(log_cum[:, None] - log_cum[None, :]) * beta_block[None, :]
        key_gram = jnp.dot(key_block, key_block.T, precision=highest)
        query_key = jnp.dot(query_block, key_block.T, precision=highest)
        lower_mix = jnp.where(strict, ratio * key_gram, 0.0)
        out_mix = jnp.where(inclusive, ratio * query_key, 0.0)
        right_side = value_block - decay_cum[:, None] * jnp.dot(key_block, state, precision=highest)
        new_values = lax.linalg.triangular_solve(
            lower_mix, right_side, left_side=True, lower=True, unit_diagonal=True
        )
        outputs = decay_cum[:, None] * jnp.dot(query_block, state, precision=highest) + jnp.dot(
            out_mix, new_values, precision=highest
        )
        weights = beta_block * jnp.exp(log_cum[-1] - log_cum)
        next_state = decay_cum[-1] * state + jnp.dot(
            key_block.T, weights[:, None] * new_values, precision=highest
        )
        return (next_state, outputs)

    final_state, outputs = lax.scan(
        span_advance, state, (query_blocks, key_blocks, value_blocks, decay_blocks, beta_blocks)
    )
    return (outputs, final_state)


def head_forward(query_head, key_head, value_pair, decay_pair, beta_pair, start_pair):
    length, width = query_head.shape
    blocks = length // SPAN
    query_blocks = (normalize(query_head) * width ** (-0.5)).reshape(blocks, SPAN, width)
    key_blocks = normalize(key_head).reshape(blocks, SPAN, width)

    def head_single(value_head, decay_head, beta_head, start_state):
        outputs, final_state = span_pass(
            query_blocks,
            key_blocks,
            value_head.reshape(blocks, SPAN, width),
            decay_head.reshape(blocks, SPAN),
            beta_head.reshape(blocks, SPAN),
            start_state,
        )
        return (outputs.reshape(length, width), final_state)

    return jax.vmap(head_single)(value_pair, decay_pair, beta_pair, start_pair)


def slab_effect(key_head, value_pair, decay_pair, beta_pair):
    length, width = key_head.shape
    blocks = length // SPAN
    key_blocks = normalize(key_head).reshape(blocks, SPAN, width)
    strict, inclusive = block_masks(SPAN)

    def slab_single(value_head, decay_head, beta_head):

        def single_advance(carried, pieces):
            state, transition = carried
            key_block, value_block, decay_log, beta_block = pieces
            log_cum = jnp.cumsum(decay_log)
            decay_cum = jnp.exp(log_cum)
            ratio = jnp.exp(log_cum[:, None] - log_cum[None, :]) * beta_block[None, :]
            key_gram = jnp.dot(key_block, key_block.T, precision=highest)
            lower_mix = jnp.where(strict, ratio * key_gram, 0.0)
            stacked = jnp.concatenate([value_block, decay_cum[:, None] * key_block], axis=1)
            solved = lax.linalg.triangular_solve(
                lower_mix, stacked, left_side=True, lower=True, unit_diagonal=True
            )
            new_values = solved[:, :width]
            mixed_keys = solved[:, width:]
            weights = beta_block * jnp.exp(log_cum[-1] - log_cum)
            weighted_keys = key_block * weights[:, None]
            next_state = decay_cum[-1] * state + jnp.dot(
                weighted_keys.T,
                new_values - jnp.dot(mixed_keys, state, precision=highest),
                precision=highest,
            )
            next_transition = decay_cum[-1] * transition - jnp.dot(
                weighted_keys.T,
                jnp.dot(mixed_keys, transition, precision=highest),
                precision=highest,
            )
            return ((next_state, next_transition), None)

        start_carry = (jnp.zeros((width, width), jnp.float32), jnp.eye(width, dtype=jnp.float32))
        (state, transition), unused = lax.scan(
            single_advance,
            start_carry,
            (
                key_blocks,
                value_head.reshape(blocks, SPAN, width),
                decay_head.reshape(blocks, SPAN),
                beta_head.reshape(blocks, SPAN),
            ),
        )
        return (transition, state)

    return jax.vmap(slab_single)(value_pair, decay_pair, beta_pair)


def start_adjoint(query_head, key_head, decay_pair, beta_pair, cot_pair):
    length, width = query_head.shape
    blocks = length // SPAN
    query_blocks = (normalize(query_head) * width ** (-0.5)).reshape(blocks, SPAN, width)
    key_blocks = normalize(key_head).reshape(blocks, SPAN, width)
    strict, inclusive = block_masks(SPAN)

    def start_single(decay_head, beta_head, cot_head):

        def retreat(grad_state, pieces):
            query_block, key_block, decay_log, beta_block, cot_block = pieces
            log_cum = jnp.cumsum(decay_log)
            decay_cum = jnp.exp(log_cum)
            ratio = jnp.exp(log_cum[:, None] - log_cum[None, :]) * beta_block[None, :]
            key_gram = jnp.dot(key_block, key_block.T, precision=highest)
            query_key = jnp.dot(query_block, key_block.T, precision=highest)
            lower_mix = jnp.where(strict, ratio * key_gram, 0.0)
            out_mix = jnp.where(inclusive, ratio * query_key, 0.0)
            mixed_keys = lax.linalg.triangular_solve(
                lower_mix,
                decay_cum[:, None] * key_block,
                left_side=True,
                lower=True,
                unit_diagonal=True,
            )
            weights = beta_block * jnp.exp(log_cum[-1] - log_cum)
            weighted_keys = key_block * weights[:, None]
            probe = decay_cum[:, None] * query_block - jnp.dot(
                out_mix, mixed_keys, precision=highest
            )
            through = decay_cum[-1] * grad_state - jnp.dot(
                mixed_keys.T,
                jnp.dot(weighted_keys, grad_state, precision=highest),
                precision=highest,
            )
            return (jnp.dot(probe.T, cot_block, precision=highest) + through, None)

        zeros_state = jnp.zeros((width, width), jnp.float32)
        result, unused = lax.scan(
            retreat,
            zeros_state,
            (
                query_blocks,
                key_blocks,
                decay_head.reshape(blocks, SPAN),
                beta_head.reshape(blocks, SPAN),
                cot_head.reshape(blocks, SPAN, width),
            ),
            reverse=True,
        )
        return result

    return jax.vmap(start_single)(decay_pair, beta_pair, cot_pair)


def matmul_states(left, right):
    return jnp.einsum("abij,abjk->abik", left, right, precision=highest)


def final_pass(
    query_head, key_head, value_pair, decay_pair, beta_pair, start_pair, cot_pair, end_pair
):

    def forward(query_in, key_in, value_in):
        return head_forward(query_in, key_in, value_in, decay_pair, beta_pair, start_pair)

    (core_out, final_unused), pullback = jax.vjp(forward, query_head, key_head, value_pair)
    return (core_out,) + pullback((cot_pair, end_pair))


def per_device(queries, keys, values, gate_code, beta_code, out_grad, w_out):
    length = queries.shape[0]
    width = HEAD_DIM
    key_count = queries.shape[1] // width
    group = values.shape[1] // queries.shape[1]
    query_heads = queries.astype(jnp.float32).reshape(length, key_count, width).transpose(1, 0, 2)
    key_heads = keys.astype(jnp.float32).reshape(length, key_count, width).transpose(1, 0, 2)
    value_heads = (
        values.astype(jnp.float32).reshape(length, key_count, group, width).transpose(1, 2, 0, 3)
    )
    decay_logs = (
        jnp.log1p(-gate_code.astype(jnp.float32) * gate_step)
        .reshape(length, key_count, group)
        .transpose(1, 2, 0)
    )
    betas = (
        (beta_code.astype(jnp.float32) / beta_steps)
        .reshape(length, key_count, group)
        .transpose(1, 2, 0)
    )
    transition, local_state = jax.vmap(slab_effect)(key_heads, value_heads, decay_logs, betas)
    full_grad = lax.all_gather(out_grad, "head", axis=1, tiled=True)
    out_cot = jnp.dot(full_grad, w_out.T, preferred_element_type=jnp.float32)
    cot_heads = out_cot.reshape(length, key_count, group, width).transpose(1, 2, 0, 3)
    empty_states = jnp.zeros_like(transition)
    carried = jax.vmap(start_adjoint)(query_heads, key_heads, decay_logs, betas, cot_heads)
    transposed = jnp.swapaxes(transition, -1, -2)
    slabs = lax.axis_size("seq")

    def forward_turn(turn, arrived):
        return from_behind(matmul_states(transition, arrived) + local_state, "seq", 1)

    start_state = lax.fori_loop(0, slabs - 1, forward_turn, empty_states)

    def backward_turn(turn, arrived):
        return from_behind(matmul_states(transposed, arrived) + carried, "seq", -1)

    end_grad = lax.fori_loop(0, slabs - 1, backward_turn, empty_states)
    core_out, query_grad, key_grad, value_grad = jax.vmap(final_pass)(
        query_heads, key_heads, value_heads, decay_logs, betas, start_state, cot_heads, end_grad
    )
    attn_out = (
        core_out.transpose(2, 0, 1, 3)
        .reshape(length, key_count * group * width)
        .astype(jnp.bfloat16)
    )
    q_grad = query_grad.transpose(1, 0, 2).reshape(length, key_count * width)
    k_grad = key_grad.transpose(1, 0, 2).reshape(length, key_count * width)
    v_grad = value_grad.transpose(2, 0, 1, 3).reshape(length, key_count * group * width)
    scaling = (length * lax.axis_size("seq")) ** (-0.5)
    weight_grad = (
        lax.psum_scatter(
            jnp.dot(attn_out.T, full_grad, preferred_element_type=jnp.float32),
            "seq",
            scatter_dimension=0,
            tiled=True,
        )
        * scaling
    )
    return (attn_out, q_grad, k_grad, v_grad, weight_grad)


def solution(mesh):
    in_specs = (
        P("seq", "head"),
        P("seq", "head"),
        P("seq", "head"),
        P("seq", "head"),
        P("seq", "head"),
        P("seq", "head"),
        P("head", None),
    )
    out_specs = (
        P("seq", "head"),
        P("seq", "head"),
        P("seq", "head"),
        P("seq", "head"),
        P(("head", "seq"), None),
    )
    return jax.shard_map(
        per_device, mesh=mesh, in_specs=in_specs, out_specs=out_specs, check_vma=False
    )
```

profile of v0, /device:TPU:15, one launch (start us, length us, event | category | flops | bytes accessed | tf_op | source)
XLA Modules:
  0.0 706.4 jit_solution(11094657248866685844)
XLA Ops:
  11.9 25.9 %while.114 = (s32[]{:T(128)}, f32[1,2,128,128]{3,2,1,0:T(8,128)S(1)}, f32[1,2,128,128]{3,2,1,0:T(8,128)S(1)}, f32[2,1,2,64]{3,2,1,0:T(2,128)S(1)}, f32[2,1,64,12...) while((s32[]{:T(128)}, ...), condition=%wide.region_3.4_spmd.clone, body=%wide.region_1.3_spmd.clone.sunk | while | flops 132489408 | bytes 2056892 | solution.py:120
  12.8 9.8 %custom-call.41 = f32[1,2,1,64,64]{3,4,2,1,0:T(8,128)S(1)} custom-call(f32[1,2,1,64,64]{4,3,2,1,0:T(8,128)S(1)} %select_add_fusion.2), custom_call_target="InvertDiagBlocksLowerTriangular" | custom-call | tf_op jit(solution)/shard_map/vmap(vmap())/while/body/eval_jaxpr/triangular_solve | solution.py:100
  25.8 9.8 %custom-call.41 = f32[1,2,1,64,64]{3,4,2,1,0:T(8,128)S(1)} custom-call(f32[1,2,1,64,64]{4,3,2,1,0:T(8,128)S(1)} %select_add_fusion.2), custom_call_target="InvertDiagBlocksLowerTriangular" | custom-call | tf_op jit(solution)/shard_map/vmap(vmap())/while/body/eval_jaxpr/triangular_solve | solution.py:100
  38.0 266.0 %while.110 = (s32[]{:T(128)}, f32[1,2,128,128]{3,2,1,0:T(8,128)S(1)}, f32[1,2,128,128]{3,2,1,0:T(8,128)S(1)}, f32[1,2,128,128]{3,2,1,0:T(8,128)S(1)}, s32[]{:T(128)}) while((s32[]{:T(128)}, f32[1,2,128,128]{3,2,1,0:T(8,128)S(1)}, f32[1,2,128,128]{3,2,1,0:T(8,128)S(1)}, f32[1,2,128,128]{3,2,1,0:T(8,128)S(1)}, s32[]{:T(128)}) %tuple.218), condition=%wide.region_5.6_spmd, body=%wide.region_4.5_spmd.sunk | while | flops 50364416 | bytes 1048677 | solution.py:237
  44.2 6.5 collective-permute-start
  61.5 6.5 collective-permute-start
  78.9 6.5 collective-permute-start
  87.5 6.5 collective-permute-start
  104.9 6.5 collective-permute-start
  113.5 6.5 collective-permute-start
  122.2 6.5 collective-permute-start
  130.9 6.5 collective-permute-start
  139.6 6.5 collective-permute-start
  156.9 6.5 collective-permute-start
  165.6 6.5 collective-permute-start
  174.2 6.5 collective-permute-start
  182.9 6.5 collective-permute-start
  191.6 6.5 collective-permute-start
  226.3 6.5 collective-permute-start
  243.6 6.5 collective-permute-start
  278.3 6.5 collective-permute-start
  295.6 6.5 collective-permute-start
  304.0 25.6 %while.113 = (s32[]{:T(128)}, f32[1,2,128,128]{3,2,1,0:T(8,128)S(1)}, bf16[2,1,2,64,128]{4,3,0,2,1:T(8,128)(2,1)S(1)}, f32[2,1,128,64]{2,3,1,0:T(8,128)S(1)}, f3...) while((s32[]{:T(128)}, ...), condition=%wide.region_9.11_spmd.clone.clone, body=%wide.region_7.10_spmd.clone.clone.sunk | while | flops 113562048 | bytes 2285849 | solution.py:57
  304.9 9.8 %custom-call.40 = f32[1,2,1,64,64]{3,4,2,1,0:T(8,128)S(1)} custom-call(f32[1,2,1,64,64]{4,3,2,1,0:T(8,128)S(1)} %add_bitcast_fusion.7), custom_call_target="InvertDiagBlocksLowerTriangular" | custom-call | tf_op jit(solution)/shard_map/vmap(jvp(vmap()))/while/body/eval_jaxpr/triangular_solve/custom-call.0 | solution.py:45
  317.8 9.8 %custom-call.40 = f32[1,2,1,64,64]{3,4,2,1,0:T(8,128)S(1)} custom-call(f32[1,2,1,64,64]{4,3,2,1,0:T(8,128)S(1)} %add_bitcast_fusion.7), custom_call_target="InvertDiagBlocksLowerTriangular" | custom-call | tf_op jit(solution)/shard_map/vmap(jvp(vmap()))/while/body/eval_jaxpr/triangular_solve/custom-call.0 | solution.py:45
  329.7 32.1 %all_gather.3 = bf16[128,2048]{1,0:T(8,128)(2,1)S(1)} all-gather(bf16[128,128]{1,0:T(8,128)(2,1)S(1)} %copy-done.3), channel_id=1, replica_groups=mesh['seq'=32,'head'=16] {'head'}, dimensions={1}, use_global_device_ids=true | all-gather | bytes 557056 | tf_op jit(solution)/shard_map/all_gather | solution.py:226
  364.3 25.8 %while.115 = (s32[]{:T(128)}, f32[1,2,128,128]{3,2,1,0:T(8,128)S(1)}, f32[2,1,2,64]{3,2,1,0:T(2,128)S(1)}, f32[2,1,64,128]{3,2,1,0:T(8,128)S(1)}, f32[2,1,2,64]{...) while((s32[]{:T(128)}, ...), condition=%wide.region_12.14_spmd.clone, body=%wide.region_10.13_spmd.clone.sunk | while | flops 113586368 | bytes 1705664 | solution.py:173
  365.2 9.8 %custom-call.42 = f32[1,2,1,64,64]{3,4,2,1,0:T(8,128)S(1)} custom-call(f32[1,2,1,64,64]{4,3,2,1,0:T(8,128)S(1)} %add_bitcast_fusion.8), custom_call_target="InvertDiagBlocksLowerTriangular" | custom-call | tf_op jit(solution)/shard_map/vmap(vmap())/while/body/eval_jaxpr/triangular_solve/custom-call.0 | solution.py:153
  378.1 9.8 %custom-call.42 = f32[1,2,1,64,64]{3,4,2,1,0:T(8,128)S(1)} custom-call(f32[1,2,1,64,64]{4,3,2,1,0:T(8,128)S(1)} %add_bitcast_fusion.8), custom_call_target="InvertDiagBlocksLowerTriangular" | custom-call | tf_op jit(solution)/shard_map/vmap(vmap())/while/body/eval_jaxpr/triangular_solve/custom-call.0 | solution.py:153
  390.2 276.1 %while.111 = (s32[]{:T(128)}, f32[1,2,128,128]{3,2,1,0:T(8,128)S(1)}, f32[1,2,128,128]{3,2,1,0:T(8,128)S(1)}, f32[1,2,128,128]{3,2,1,0:T(8,128)S(1)}, s32[]{:T(128)}) while((s32[]{:T(128)}, f32[1,2,128,128]{3,2,1,0:T(8,128)S(1)}, f32[1,2,128,128]{3,2,1,0:T(8,128)S(1)}, f32[1,2,128,128]{3,2,1,0:T(8,128)S(1)}, s32[]{:T(128)}) %tuple.227), condition=%wide.region_14.16_spmd, body=%wide.region_13.15_spmd.sunk | while | flops 50364416 | bytes 1048677 | solution.py:242
  393.8 12.0 %collective-permute-done.1 = f32[1,2,128,128]{3,2,1,0:T(8,128)S(1)} collective-permute-done((f32[1,2,128,128]{3,2,1,0:T(8,128)S(1)}, f32[1,2,128,128]{3,2,1,0:T(8,128)S(1)}, u32[]{:S(2)}, u32[]{:S(2)}) %collective-permute-start.1) | collective-permute-done | bytes 131104 | tf_op jit(solution)/shard_map/while/body/eval_jaxpr/ppermute | solution.py:17
  408.0 6.5 collective-permute-done.1
  416.7 6.5 collective-permute-done.1
  425.4 6.5 collective-permute-done.1
  434.1 6.5 collective-permute-done.1
  442.7 6.5 collective-permute-done.1
  451.4 6.6 collective-permute-done.1
  460.3 6.6 collective-permute-done.1
  469.1 6.5 collective-permute-done.1
  477.8 6.5 collective-permute-done.1
  486.4 6.5 collective-permute-done.1
  495.1 6.5 collective-permute-done.1
  503.8 6.5 collective-permute-done.1
  512.5 6.5 collective-permute-done.1
  521.1 6.5 collective-permute-done.1
  529.8 6.5 collective-permute-done.1
  538.5 6.5 collective-permute-done.1
  547.1 6.5 collective-permute-done.1
  555.8 6.5 collective-permute-done.1
  564.5 6.5 collective-permute-done.1
  573.2 6.5 collective-permute-done.1
  581.8 6.5 collective-permute-done.1
  590.5 6.5 collective-permute-done.1
  599.2 6.5 collective-permute-done.1
  607.8 6.5 collective-permute-done.1
  616.5 6.5 collective-permute-done.1
  625.2 6.5 collective-permute-done.1
  633.8 6.5 collective-permute-done.1
  642.5 6.5 collective-permute-done.1
  651.2 6.5 collective-permute-done.1
  659.9 6.5 collective-permute-done.1
  666.6 28.2 %while.112 = (s32[]{:T(128)}, f32[1,2,128,128]{2,3,1,0:T(8,128)S(1)}, f32[2,1,64,128]{3,2,1,0:T(8,128)S(1)}, f32[2,1,64,128]{3,2,1,0:T(8,128)S(1)}, f32[2,1,2,64...) while((s32[]{:T(128)}, ...), condition=%wide.region_18.20_spmd.clone, body=%wide.region_15.19_spmd.clone.sunk | while | flops 233140288 | bytes 3349265 | solution.py:57
  667.3 9.8 %custom-call.39 = f32[1,2,1,64,64]{3,4,2,1,0:T(8,128)S(1)} custom-call(f32[1,2,1,64,64]{4,3,2,1,0:T(8,128)S(1)} %add_bitcast_fusion.6), custom_call_target="InvertDiagBlocksLowerTriangular" | custom-call | tf_op jit(solution)/shard_map/vmap(transpose(jvp(vmap())))/while/body/eval_jaxpr/triangular_solve | solution.py:45
  681.4 9.8 %custom-call.39 = f32[1,2,1,64,64]{3,4,2,1,0:T(8,128)S(1)} custom-call(f32[1,2,1,64,64]{4,3,2,1,0:T(8,128)S(1)} %add_bitcast_fusion.6), custom_call_target="InvertDiagBlocksLowerTriangular" | custom-call | tf_op jit(solution)/shard_map/vmap(transpose(jvp(vmap())))/while/body/eval_jaxpr/triangular_solve | solution.py:45
  (363 shorter events, 256.4 us)
Async XLA Ops:
  7.2 356.5 %copy-start = (bf16[256,2048]{1,0:T(8,128)(2,1)S(1)}, bf16[256,2048]{1,0:T(8,128)(2,1)}, u32[]{:S(2)}) copy-start(bf16[256,2048]{1,0:T(8,128)(2,1)} %param.27) | copy-start | bytes 3145732
  7.2 690.9 %reduce-scatter.2.cloned.1.call-start = ((), (), s32[]{:S(2)}) async-start(), calls=%async_computation.1 | async-start | bytes 2162688 | tf_op jit(solution)/shard_map/reduce_scatter | solution.py:256
  38.3 5.6 collective-permute-start
  44.2 8.4 %collective-permute-start = (f32[1,2,128,128]{3,2,1,0:T(8,128)S(1)}, f32[1,2,128,128]{3,2,1,0:T(8,128)S(1)}, u32[]{:S(2)}, u32[]{:S(2)}) collective-permute-start(f32[1,2,128,128]{3,2,1,0:T(8,128)S(1)} %fusion.351), channel_id=1, source_target_pairs={{0,16},{16,32},{32,48},{48,64},{64,80},{80,96},{96,112},{112,128},... | collective-permute-start | bytes 393224 | tf_op jit(solution)/shard_map/while/body/eval_jaxpr/ppermute | solution.py:17
  52.9 8.4 %collective-permute-start = (f32[1,2,128,128]{3,2,1,0:T(8,128)S(1)}, f32[1,2,128,128]{3,2,1,0:T(8,128)S(1)}, u32[]{:S(2)}, u32[]{:S(2)}) collective-permute-start(f32[1,2,128,128]{3,2,1,0:T(8,128)S(1)} %fusion.351), channel_id=1, source_target_pairs={{0,16},{16,32},{32,48},{48,64},{64,80},{80,96},{96,112},{112,128},... | collective-permute-start | bytes 393224 | tf_op jit(solution)/shard_map/while/body/eval_jaxpr/ppermute | solution.py:17
  61.5 8.4 %collective-permute-start = (f32[1,2,128,128]{3,2,1,0:T(8,128)S(1)}, f32[1,2,128,128]{3,2,1,0:T(8,128)S(1)}, u32[]{:S(2)}, u32[]{:S(2)}) collective-permute-start(f32[1,2,128,128]{3,2,1,0:T(8,128)S(1)} %fusion.351), channel_id=1, source_target_pairs={{0,16},{16,32},{32,48},{48,64},{64,80},{80,96},{96,112},{112,128},... | collective-permute-start | bytes 393224 | tf_op jit(solution)/shard_map/while/body/eval_jaxpr/ppermute | solution.py:17
  70.2 8.4 %collective-permute-start = (f32[1,2,128,128]{3,2,1,0:T(8,128)S(1)}, f32[1,2,128,128]{3,2,1,0:T(8,128)S(1)}, u32[]{:S(2)}, u32[]{:S(2)}) collective-permute-start(f32[1,2,128,128]{3,2,1,0:T(8,128)S(1)} %fusion.351), channel_id=1, source_target_pairs={{0,16},{16,32},{32,48},{48,64},{64,80},{80,96},{96,112},{112,128},... | collective-permute-start | bytes 393224 | tf_op jit(solution)/shard_map/while/body/eval_jaxpr/ppermute | solution.py:17
  78.9 8.4 %collective-permute-start = (f32[1,2,128,128]{3,2,1,0:T(8,128)S(1)}, f32[1,2,128,128]{3,2,1,0:T(8,128)S(1)}, u32[]{:S(2)}, u32[]{:S(2)}) collective-permute-start(f32[1,2,128,128]{3,2,1,0:T(8,128)S(1)} %fusion.351), channel_id=1, source_target_pairs={{0,16},{16,32},{32,48},{48,64},{64,80},{80,96},{96,112},{112,128},... | collective-permute-start | bytes 393224 | tf_op jit(solution)/shard_map/while/body/eval_jaxpr/ppermute | solution.py:17
  87.5 8.4 %collective-permute-start = (f32[1,2,128,128]{3,2,1,0:T(8,128)S(1)}, f32[1,2,128,128]{3,2,1,0:T(8,128)S(1)}, u32[]{:S(2)}, u32[]{:S(2)}) collective-permute-start(f32[1,2,128,128]{3,2,1,0:T(8,128)S(1)} %fusion.351), channel_id=1, source_target_pairs={{0,16},{16,32},{32,48},{48,64},{64,80},{80,96},{96,112},{112,128},... | collective-permute-start | bytes 393224 | tf_op jit(solution)/shard_map/while/body/eval_jaxpr/ppermute | solution.py:17
  96.2 8.4 %collective-permute-start = (f32[1,2,128,128]{3,2,1,0:T(8,128)S(1)}, f32[1,2,128,128]{3,2,1,0:T(8,128)S(1)}, u32[]{:S(2)}, u32[]{:S(2)}) collective-permute-start(f32[1,2,128,128]{3,2,1,0:T(8,128)S(1)} %fusion.351), channel_id=1, source_target_pairs={{0,16},{16,32},{32,48},{48,64},{64,80},{80,96},{96,112},{112,128},... | collective-permute-start | bytes 393224 | tf_op jit(solution)/shard_map/while/body/eval_jaxpr/ppermute | solution.py:17
  104.9 8.4 %collective-permute-start = (f32[1,2,128,128]{3,2,1,0:T(8,128)S(1)}, f32[1,2,128,128]{3,2,1,0:T(8,128)S(1)}, u32[]{:S(2)}, u32[]{:S(2)}) collective-permute-start(f32[1,2,128,128]{3,2,1,0:T(8,128)S(1)} %fusion.351), channel_id=1, source_target_pairs={{0,16},{16,32},{32,48},{48,64},{64,80},{80,96},{96,112},{112,128},... | collective-permute-start | bytes 393224 | tf_op jit(solution)/shard_map/while/body/eval_jaxpr/ppermute | solution.py:17
  113.5 8.4 %collective-permute-start = (f32[1,2,128,128]{3,2,1,0:T(8,128)S(1)}, f32[1,2,128,128]{3,2,1,0:T(8,128)S(1)}, u32[]{:S(2)}, u32[]{:S(2)}) collective-permute-start(f32[1,2,128,128]{3,2,1,0:T(8,128)S(1)} %fusion.351), channel_id=1, source_target_pairs={{0,16},{16,32},{32,48},{48,64},{64,80},{80,96},{96,112},{112,128},... | collective-permute-start | bytes 393224 | tf_op jit(solution)/shard_map/while/body/eval_jaxpr/ppermute | solution.py:17
  122.2 8.4 %collective-permute-start = (f32[1,2,128,128]{3,2,1,0:T(8,128)S(1)}, f32[1,2,128,128]{3,2,1,0:T(8,128)S(1)}, u32[]{:S(2)}, u32[]{:S(2)}) collective-permute-start(f32[1,2,128,128]{3,2,1,0:T(8,128)S(1)} %fusion.351), channel_id=1, source_target_pairs={{0,16},{16,32},{32,48},{48,64},{64,80},{80,96},{96,112},{112,128},... | collective-permute-start | bytes 393224 | tf_op jit(solution)/shard_map/while/body/eval_jaxpr/ppermute | solution.py:17
  130.9 8.4 %collective-permute-start = (f32[1,2,128,128]{3,2,1,0:T(8,128)S(1)}, f32[1,2,128,128]{3,2,1,0:T(8,128)S(1)}, u32[]{:S(2)}, u32[]{:S(2)}) collective-permute-start(f32[1,2,128,128]{3,2,1,0:T(8,128)S(1)} %fusion.351), channel_id=1, source_target_pairs={{0,16},{16,32},{32,48},{48,64},{64,80},{80,96},{96,112},{112,128},... | collective-permute-start | bytes 393224 | tf_op jit(solution)/shard_map/while/body/eval_jaxpr/ppermute | solution.py:17
  139.6 8.4 %collective-permute-start = (f32[1,2,128,128]{3,2,1,0:T(8,128)S(1)}, f32[1,2,128,128]{3,2,1,0:T(8,128)S(1)}, u32[]{:S(2)}, u32[]{:S(2)}) collective-permute-start(f32[1,2,128,128]{3,2,1,0:T(8,128)S(1)} %fusion.351), channel_id=1, source_target_pairs={{0,16},{16,32},{32,48},{48,64},{64,80},{80,96},{96,112},{112,128},... | collective-permute-start | bytes 393224 | tf_op jit(solution)/shard_map/while/body/eval_jaxpr/ppermute | solution.py:17
  148.2 8.4 %collective-permute-start = (f32[1,2,128,128]{3,2,1,0:T(8,128)S(1)}, f32[1,2,128,128]{3,2,1,0:T(8,128)S(1)}, u32[]{:S(2)}, u32[]{:S(2)}) collective-permute-start(f32[1,2,128,128]{3,2,1,0:T(8,128)S(1)} %fusion.351), channel_id=1, source_target_pairs={{0,16},{16,32},{32,48},{48,64},{64,80},{80,96},{96,112},{112,128},... | collective-permute-start | bytes 393224 | tf_op jit(solution)/shard_map/while/body/eval_jaxpr/ppermute | solution.py:17
  156.9 8.4 %collective-permute-start = (f32[1,2,128,128]{3,2,1,0:T(8,128)S(1)}, f32[1,2,128,128]{3,2,1,0:T(8,128)S(1)}, u32[]{:S(2)}, u32[]{:S(2)}) collective-permute-start(f32[1,2,128,128]{3,2,1,0:T(8,128)S(1)} %fusion.351), channel_id=1, source_target_pairs={{0,16},{16,32},{32,48},{48,64},{64,80},{80,96},{96,112},{112,128},... | collective-permute-start | bytes 393224 | tf_op jit(solution)/shard_map/while/body/eval_jaxpr/ppermute | solution.py:17
  165.6 8.4 %collective-permute-start = (f32[1,2,128,128]{3,2,1,0:T(8,128)S(1)}, f32[1,2,128,128]{3,2,1,0:T(8,128)S(1)}, u32[]{:S(2)}, u32[]{:S(2)}) collective-permute-start(f32[1,2,128,128]{3,2,1,0:T(8,128)S(1)} %fusion.351), channel_id=1, source_target_pairs={{0,16},{16,32},{32,48},{48,64},{64,80},{80,96},{96,112},{112,128},... | collective-permute-start | bytes 393224 | tf_op jit(solution)/shard_map/while/body/eval_jaxpr/ppermute | solution.py:17
  174.2 8.4 %collective-permute-start = (f32[1,2,128,128]{3,2,1,0:T(8,128)S(1)}, f32[1,2,128,128]{3,2,1,0:T(8,128)S(1)}, u32[]{:S(2)}, u32[]{:S(2)}) collective-permute-start(f32[1,2,128,128]{3,2,1,0:T(8,128)S(1)} %fusion.351), channel_id=1, source_target_pairs={{0,16},{16,32},{32,48},{48,64},{64,80},{80,96},{96,112},{112,128},... | collective-permute-start | bytes 393224 | tf_op jit(solution)/shard_map/while/body/eval_jaxpr/ppermute | solution.py:17
  182.9 8.4 %collective-permute-start = (f32[1,2,128,128]{3,2,1,0:T(8,128)S(1)}, f32[1,2,128,128]{3,2,1,0:T(8,128)S(1)}, u32[]{:S(2)}, u32[]{:S(2)}) collective-permute-start(f32[1,2,128,128]{3,2,1,0:T(8,128)S(1)} %fusion.351), channel_id=1, source_target_pairs={{0,16},{16,32},{32,48},{48,64},{64,80},{80,96},{96,112},{112,128},... | collective-permute-start | bytes 393224 | tf_op jit(solution)/shard_map/while/body/eval_jaxpr/ppermute | solution.py:17
  191.6 8.4 %collective-permute-start = (f32[1,2,128,128]{3,2,1,0:T(8,128)S(1)}, f32[1,2,128,128]{3,2,1,0:T(8,128)S(1)}, u32[]{:S(2)}, u32[]{:S(2)}) collective-permute-start(f32[1,2,128,128]{3,2,1,0:T(8,128)S(1)} %fusion.351), channel_id=1, source_target_pairs={{0,16},{16,32},{32,48},{48,64},{64,80},{80,96},{96,112},{112,128},... | collective-permute-start | bytes 393224 | tf_op jit(solution)/shard_map/while/body/eval_jaxpr/ppermute | solution.py:17
  200.3 8.4 %collective-permute-start = (f32[1,2,128,128]{3,2,1,0:T(8,128)S(1)}, f32[1,2,128,128]{3,2,1,0:T(8,128)S(1)}, u32[]{:S(2)}, u32[]{:S(2)}) collective-permute-start(f32[1,2,128,128]{3,2,1,0:T(8,128)S(1)} %fusion.351), channel_id=1, source_target_pairs={{0,16},{16,32},{32,48},{48,64},{64,80},{80,96},{96,112},{112,128},... | collective-permute-start | bytes 393224 | tf_op jit(solution)/shard_map/while/body/eval_jaxpr/ppermute | solution.py:17
  208.9 8.4 %collective-permute-start = (f32[1,2,128,128]{3,2,1,0:T(8,128)S(1)}, f32[1,2,128,128]{3,2,1,0:T(8,128)S(1)}, u32[]{:S(2)}, u32[]{:S(2)}) collective-permute-start(f32[1,2,128,128]{3,2,1,0:T(8,128)S(1)} %fusion.351), channel_id=1, source_target_pairs={{0,16},{16,32},{32,48},{48,64},{64,80},{80,96},{96,112},{112,128},... | collective-permute-start | bytes 393224 | tf_op jit(solution)/shard_map/while/body/eval_jaxpr/ppermute | solution.py:17
  217.6 8.4 %collective-permute-start = (f32[1,2,128,128]{3,2,1,0:T(8,128)S(1)}, f32[1,2,128,128]{3,2,1,0:T(8,128)S(1)}, u32[]{:S(2)}, u32[]{:S(2)}) collective-permute-start(f32[1,2,128,128]{3,2,1,0:T(8,128)S(1)} %fusion.351), channel_id=1, source_target_pairs={{0,16},{16,32},{32,48},{48,64},{64,80},{80,96},{96,112},{112,128},... | collective-permute-start | bytes 393224 | tf_op jit(solution)/shard_map/while/body/eval_jaxpr/ppermute | solution.py:17
  226.3 8.4 %collective-permute-start = (f32[1,2,128,128]{3,2,1,0:T(8,128)S(1)}, f32[1,2,128,128]{3,2,1,0:T(8,128)S(1)}, u32[]{:S(2)}, u32[]{:S(2)}) collective-permute-start(f32[1,2,128,128]{3,2,1,0:T(8,128)S(1)} %fusion.351), channel_id=1, source_target_pairs={{0,16},{16,32},{32,48},{48,64},{64,80},{80,96},{96,112},{112,128},... | collective-permute-start | bytes 393224 | tf_op jit(solution)/shard_map/while/body/eval_jaxpr/ppermute | solution.py:17
  234.9 8.4 %collective-permute-start = (f32[1,2,128,128]{3,2,1,0:T(8,128)S(1)}, f32[1,2,128,128]{3,2,1,0:T(8,128)S(1)}, u32[]{:S(2)}, u32[]{:S(2)}) collective-permute-start(f32[1,2,128,128]{3,2,1,0:T(8,128)S(1)} %fusion.351), channel_id=1, source_target_pairs={{0,16},{16,32},{32,48},{48,64},{64,80},{80,96},{96,112},{112,128},... | collective-permute-start | bytes 393224 | tf_op jit(solution)/shard_map/while/body/eval_jaxpr/ppermute | solution.py:17
  243.6 8.4 %collective-permute-start = (f32[1,2,128,128]{3,2,1,0:T(8,128)S(1)}, f32[1,2,128,128]{3,2,1,0:T(8,128)S(1)}, u32[]{:S(2)}, u32[]{:S(2)}) collective-permute-start(f32[1,2,128,128]{3,2,1,0:T(8,128)S(1)} %fusion.351), channel_id=1, source_target_pairs={{0,16},{16,32},{32,48},{48,64},{64,80},{80,96},{96,112},{112,128},... | collective-permute-start | bytes 393224 | tf_op jit(solution)/shard_map/while/body/eval_jaxpr/ppermute | solution.py:17
  252.3 8.4 %collective-permute-start = (f32[1,2,128,128]{3,2,1,0:T(8,128)S(1)}, f32[1,2,128,128]{3,2,1,0:T(8,128)S(1)}, u32[]{:S(2)}, u32[]{:S(2)}) collective-permute-start(f32[1,2,128,128]{3,2,1,0:T(8,128)S(1)} %fusion.351), channel_id=1, source_target_pairs={{0,16},{16,32},{32,48},{48,64},{64,80},{80,96},{96,112},{112,128},... | collective-permute-start | bytes 393224 | tf_op jit(solution)/shard_map/while/body/eval_jaxpr/ppermute | solution.py:17
  261.0 8.4 %collective-permute-start = (f32[1,2,128,128]{3,2,1,0:T(8,128)S(1)}, f32[1,2,128,128]{3,2,1,0:T(8,128)S(1)}, u32[]{:S(2)}, u32[]{:S(2)}) collective-permute-start(f32[1,2,128,128]{3,2,1,0:T(8,128)S(1)} %fusion.351), channel_id=1, source_target_pairs={{0,16},{16,32},{32,48},{48,64},{64,80},{80,96},{96,112},{112,128},... | collective-permute-start | bytes 393224 | tf_op jit(solution)/shard_map/while/body/eval_jaxpr/ppermute | solution.py:17
  269.6 8.4 %collective-permute-start = (f32[1,2,128,128]{3,2,1,0:T(8,128)S(1)}, f32[1,2,128,128]{3,2,1,0:T(8,128)S(1)}, u32[]{:S(2)}, u32[]{:S(2)}) collective-permute-start(f32[1,2,128,128]{3,2,1,0:T(8,128)S(1)} %fusion.351), channel_id=1, source_target_pairs={{0,16},{16,32},{32,48},{48,64},{64,80},{80,96},{96,112},{112,128},... | collective-permute-start | bytes 393224 | tf_op jit(solution)/shard_map/while/body/eval_jaxpr/ppermute | solution.py:17
  278.3 8.4 %collective-permute-start = (f32[1,2,128,128]{3,2,1,0:T(8,128)S(1)}, f32[1,2,128,128]{3,2,1,0:T(8,128)S(1)}, u32[]{:S(2)}, u32[]{:S(2)}) collective-permute-start(f32[1,2,128,128]{3,2,1,0:T(8,128)S(1)} %fusion.351), channel_id=1, source_target_pairs={{0,16},{16,32},{32,48},{48,64},{64,80},{80,96},{96,112},{112,128},... | collective-permute-start | bytes 393224 | tf_op jit(solution)/shard_map/while/body/eval_jaxpr/ppermute | solution.py:17
  287.0 8.4 %collective-permute-start = (f32[1,2,128,128]{3,2,1,0:T(8,128)S(1)}, f32[1,2,128,128]{3,2,1,0:T(8,128)S(1)}, u32[]{:S(2)}, u32[]{:S(2)}) collective-permute-start(f32[1,2,128,128]{3,2,1,0:T(8,128)S(1)} %fusion.351), channel_id=1, source_target_pairs={{0,16},{16,32},{32,48},{48,64},{64,80},{80,96},{96,112},{112,128},... | collective-permute-start | bytes 393224 | tf_op jit(solution)/shard_map/while/body/eval_jaxpr/ppermute | solution.py:17
  295.6 8.4 %collective-permute-start = (f32[1,2,128,128]{3,2,1,0:T(8,128)S(1)}, f32[1,2,128,128]{3,2,1,0:T(8,128)S(1)}, u32[]{:S(2)}, u32[]{:S(2)}) collective-permute-start(f32[1,2,128,128]{3,2,1,0:T(8,128)S(1)} %fusion.351), channel_id=1, source_target_pairs={{0,16},{16,32},{32,48},{48,64},{64,80},{80,96},{96,112},{112,128},... | collective-permute-start | bytes 393224 | tf_op jit(solution)/shard_map/while/body/eval_jaxpr/ppermute | solution.py:17
  390.5 15.3 %collective-permute-start.1 = (f32[1,2,128,128]{3,2,1,0:T(8,128)S(1)}, f32[1,2,128,128]{3,2,1,0:T(8,128)S(1)}, u32[]{:S(2)}, u32[]{:S(2)}) collective-permute-start(f32[1,2,128,128]{3,2,1,0:T(8,128)S(1)} %fusion.354), channel_id=1, source_target_pairs={{16,0},{32,16},{48,32},{64,48},{80,64},{96,80},{112,96},{128,112},... | collective-permute-start | bytes 393224 | tf_op jit(solution)/shard_map/while/body/eval_jaxpr/ppermute | solution.py:17
  406.1 8.4 %collective-permute-start.1 = (f32[1,2,128,128]{3,2,1,0:T(8,128)S(1)}, f32[1,2,128,128]{3,2,1,0:T(8,128)S(1)}, u32[]{:S(2)}, u32[]{:S(2)}) collective-permute-start(f32[1,2,128,128]{3,2,1,0:T(8,128)S(1)} %fusion.354), channel_id=1, source_target_pairs={{16,0},{32,16},{48,32},{64,48},{80,64},{96,80},{112,96},{128,112},... | collective-permute-start | bytes 393224 | tf_op jit(solution)/shard_map/while/body/eval_jaxpr/ppermute | solution.py:17
  414.8 8.4 %collective-permute-start.1 = (f32[1,2,128,128]{3,2,1,0:T(8,128)S(1)}, f32[1,2,128,128]{3,2,1,0:T(8,128)S(1)}, u32[]{:S(2)}, u32[]{:S(2)}) collective-permute-start(f32[1,2,128,128]{3,2,1,0:T(8,128)S(1)} %fusion.354), channel_id=1, source_target_pairs={{16,0},{32,16},{48,32},{64,48},{80,64},{96,80},{112,96},{128,112},... | collective-permute-start | bytes 393224 | tf_op jit(solution)/shard_map/while/body/eval_jaxpr/ppermute | solution.py:17
  423.4 8.4 %collective-permute-start.1 = (f32[1,2,128,128]{3,2,1,0:T(8,128)S(1)}, f32[1,2,128,128]{3,2,1,0:T(8,128)S(1)}, u32[]{:S(2)}, u32[]{:S(2)}) collective-permute-start(f32[1,2,128,128]{3,2,1,0:T(8,128)S(1)} %fusion.354), channel_id=1, source_target_pairs={{16,0},{32,16},{48,32},{64,48},{80,64},{96,80},{112,96},{128,112},... | collective-permute-start | bytes 393224 | tf_op jit(solution)/shard_map/while/body/eval_jaxpr/ppermute | solution.py:17
  432.1 8.4 %collective-permute-start.1 = (f32[1,2,128,128]{3,2,1,0:T(8,128)S(1)}, f32[1,2,128,128]{3,2,1,0:T(8,128)S(1)}, u32[]{:S(2)}, u32[]{:S(2)}) collective-permute-start(f32[1,2,128,128]{3,2,1,0:T(8,128)S(1)} %fusion.354), channel_id=1, source_target_pairs={{16,0},{32,16},{48,32},{64,48},{80,64},{96,80},{112,96},{128,112},... | collective-permute-start | bytes 393224 | tf_op jit(solution)/shard_map/while/body/eval_jaxpr/ppermute | solution.py:17
  440.8 8.4 %collective-permute-start.1 = (f32[1,2,128,128]{3,2,1,0:T(8,128)S(1)}, f32[1,2,128,128]{3,2,1,0:T(8,128)S(1)}, u32[]{:S(2)}, u32[]{:S(2)}) collective-permute-start(f32[1,2,128,128]{3,2,1,0:T(8,128)S(1)} %fusion.354), channel_id=1, source_target_pairs={{16,0},{32,16},{48,32},{64,48},{80,64},{96,80},{112,96},{128,112},... | collective-permute-start | bytes 393224 | tf_op jit(solution)/shard_map/while/body/eval_jaxpr/ppermute | solution.py:17
  449.5 8.6 %collective-permute-start.1 = (f32[1,2,128,128]{3,2,1,0:T(8,128)S(1)}, f32[1,2,128,128]{3,2,1,0:T(8,128)S(1)}, u32[]{:S(2)}, u32[]{:S(2)}) collective-permute-start(f32[1,2,128,128]{3,2,1,0:T(8,128)S(1)} %fusion.354), channel_id=1, source_target_pairs={{16,0},{32,16},{48,32},{64,48},{80,64},{96,80},{112,96},{128,112},... | collective-permute-start | bytes 393224 | tf_op jit(solution)/shard_map/while/body/eval_jaxpr/ppermute | solution.py:17
  458.3 8.6 %collective-permute-start.1 = (f32[1,2,128,128]{3,2,1,0:T(8,128)S(1)}, f32[1,2,128,128]{3,2,1,0:T(8,128)S(1)}, u32[]{:S(2)}, u32[]{:S(2)}) collective-permute-start(f32[1,2,128,128]{3,2,1,0:T(8,128)S(1)} %fusion.354), channel_id=1, source_target_pairs={{16,0},{32,16},{48,32},{64,48},{80,64},{96,80},{112,96},{128,112},... | collective-permute-start | bytes 393224 | tf_op jit(solution)/shard_map/while/body/eval_jaxpr/ppermute | solution.py:17
  467.2 8.4 %collective-permute-start.1 = (f32[1,2,128,128]{3,2,1,0:T(8,128)S(1)}, f32[1,2,128,128]{3,2,1,0:T(8,128)S(1)}, u32[]{:S(2)}, u32[]{:S(2)}) collective-permute-start(f32[1,2,128,128]{3,2,1,0:T(8,128)S(1)} %fusion.354), channel_id=1, source_target_pairs={{16,0},{32,16},{48,32},{64,48},{80,64},{96,80},{112,96},{128,112},... | collective-permute-start | bytes 393224 | tf_op jit(solution)/shard_map/while/body/eval_jaxpr/ppermute | solution.py:17
  475.8 8.4 %collective-permute-start.1 = (f32[1,2,128,128]{3,2,1,0:T(8,128)S(1)}, f32[1,2,128,128]{3,2,1,0:T(8,128)S(1)}, u32[]{:S(2)}, u32[]{:S(2)}) collective-permute-start(f32[1,2,128,128]{3,2,1,0:T(8,128)S(1)} %fusion.354), channel_id=1, source_target_pairs={{16,0},{32,16},{48,32},{64,48},{80,64},{96,80},{112,96},{128,112},... | collective-permute-start | bytes 393224 | tf_op jit(solution)/shard_map/while/body/eval_jaxpr/ppermute | solution.py:17
  484.5 8.4 %collective-permute-start.1 = (f32[1,2,128,128]{3,2,1,0:T(8,128)S(1)}, f32[1,2,128,128]{3,2,1,0:T(8,128)S(1)}, u32[]{:S(2)}, u32[]{:S(2)}) collective-permute-start(f32[1,2,128,128]{3,2,1,0:T(8,128)S(1)} %fusion.354), channel_id=1, source_target_pairs={{16,0},{32,16},{48,32},{64,48},{80,64},{96,80},{112,96},{128,112},... | collective-permute-start | bytes 393224 | tf_op jit(solution)/shard_map/while/body/eval_jaxpr/ppermute | solution.py:17
  493.2 8.4 %collective-permute-start.1 = (f32[1,2,128,128]{3,2,1,0:T(8,128)S(1)}, f32[1,2,128,128]{3,2,1,0:T(8,128)S(1)}, u32[]{:S(2)}, u32[]{:S(2)}) collective-permute-start(f32[1,2,128,128]{3,2,1,0:T(8,128)S(1)} %fusion.354), channel_id=1, source_target_pairs={{16,0},{32,16},{48,32},{64,48},{80,64},{96,80},{112,96},{128,112},... | collective-permute-start | bytes 393224 | tf_op jit(solution)/shard_map/while/body/eval_jaxpr/ppermute | solution.py:17
  501.9 8.4 %collective-permute-start.1 = (f32[1,2,128,128]{3,2,1,0:T(8,128)S(1)}, f32[1,2,128,128]{3,2,1,0:T(8,128)S(1)}, u32[]{:S(2)}, u32[]{:S(2)}) collective-permute-start(f32[1,2,128,128]{3,2,1,0:T(8,128)S(1)} %fusion.354), channel_id=1, source_target_pairs={{16,0},{32,16},{48,32},{64,48},{80,64},{96,80},{112,96},{128,112},... | collective-permute-start | bytes 393224 | tf_op jit(solution)/shard_map/while/body/eval_jaxpr/ppermute | solution.py:17
  510.5 8.4 %collective-permute-start.1 = (f32[1,2,128,128]{3,2,1,0:T(8,128)S(1)}, f32[1,2,128,128]{3,2,1,0:T(8,128)S(1)}, u32[]{:S(2)}, u32[]{:S(2)}) collective-permute-start(f32[1,2,128,128]{3,2,1,0:T(8,128)S(1)} %fusion.354), channel_id=1, source_target_pairs={{16,0},{32,16},{48,32},{64,48},{80,64},{96,80},{112,96},{128,112},... | collective-permute-start | bytes 393224 | tf_op jit(solution)/shard_map/while/body/eval_jaxpr/ppermute | solution.py:17
  519.2 8.4 %collective-permute-start.1 = (f32[1,2,128,128]{3,2,1,0:T(8,128)S(1)}, f32[1,2,128,128]{3,2,1,0:T(8,128)S(1)}, u32[]{:S(2)}, u32[]{:S(2)}) collective-permute-start(f32[1,2,128,128]{3,2,1,0:T(8,128)S(1)} %fusion.354), channel_id=1, source_target_pairs={{16,0},{32,16},{48,32},{64,48},{80,64},{96,80},{112,96},{128,112},... | collective-permute-start | bytes 393224 | tf_op jit(solution)/shard_map/while/body/eval_jaxpr/ppermute | solution.py:17
  527.9 8.4 %collective-permute-start.1 = (f32[1,2,128,128]{3,2,1,0:T(8,128)S(1)}, f32[1,2,128,128]{3,2,1,0:T(8,128)S(1)}, u32[]{:S(2)}, u32[]{:S(2)}) collective-permute-start(f32[1,2,128,128]{3,2,1,0:T(8,128)S(1)} %fusion.354), channel_id=1, source_target_pairs={{16,0},{32,16},{48,32},{64,48},{80,64},{96,80},{112,96},{128,112},... | collective-permute-start | bytes 393224 | tf_op jit(solution)/shard_map/while/body/eval_jaxpr/ppermute | solution.py:17
  536.5 8.4 %collective-permute-start.1 = (f32[1,2,128,128]{3,2,1,0:T(8,128)S(1)}, f32[1,2,128,128]{3,2,1,0:T(8,128)S(1)}, u32[]{:S(2)}, u32[]{:S(2)}) collective-permute-start(f32[1,2,128,128]{3,2,1,0:T(8,128)S(1)} %fusion.354), channel_id=1, source_target_pairs={{16,0},{32,16},{48,32},{64,48},{80,64},{96,80},{112,96},{128,112},... | collective-permute-start | bytes 393224 | tf_op jit(solution)/shard_map/while/body/eval_jaxpr/ppermute | solution.py:17
  545.2 8.4 %collective-permute-start.1 = (f32[1,2,128,128]{3,2,1,0:T(8,128)S(1)}, f32[1,2,128,128]{3,2,1,0:T(8,128)S(1)}, u32[]{:S(2)}, u32[]{:S(2)}) collective-permute-start(f32[1,2,128,128]{3,2,1,0:T(8,128)S(1)} %fusion.354), channel_id=1, source_target_pairs={{16,0},{32,16},{48,32},{64,48},{80,64},{96,80},{112,96},{128,112},... | collective-permute-start | bytes 393224 | tf_op jit(solution)/shard_map/while/body/eval_jaxpr/ppermute | solution.py:17
  553.9 8.4 %collective-permute-start.1 = (f32[1,2,128,128]{3,2,1,0:T(8,128)S(1)}, f32[1,2,128,128]{3,2,1,0:T(8,128)S(1)}, u32[]{:S(2)}, u32[]{:S(2)}) collective-permute-start(f32[1,2,128,128]{3,2,1,0:T(8,128)S(1)} %fusion.354), channel_id=1, source_target_pairs={{16,0},{32,16},{48,32},{64,48},{80,64},{96,80},{112,96},{128,112},... | collective-permute-start | bytes 393224 | tf_op jit(solution)/shard_map/while/body/eval_jaxpr/ppermute | solution.py:17
  562.5 8.4 %collective-permute-start.1 = (f32[1,2,128,128]{3,2,1,0:T(8,128)S(1)}, f32[1,2,128,128]{3,2,1,0:T(8,128)S(1)}, u32[]{:S(2)}, u32[]{:S(2)}) collective-permute-start(f32[1,2,128,128]{3,2,1,0:T(8,128)S(1)} %fusion.354), channel_id=1, source_target_pairs={{16,0},{32,16},{48,32},{64,48},{80,64},{96,80},{112,96},{128,112},... | collective-permute-start | bytes 393224 | tf_op jit(solution)/shard_map/while/body/eval_jaxpr/ppermute | solution.py:17
  571.2 8.4 %collective-permute-start.1 = (f32[1,2,128,128]{3,2,1,0:T(8,128)S(1)}, f32[1,2,128,128]{3,2,1,0:T(8,128)S(1)}, u32[]{:S(2)}, u32[]{:S(2)}) collective-permute-start(f32[1,2,128,128]{3,2,1,0:T(8,128)S(1)} %fusion.354), channel_id=1, source_target_pairs={{16,0},{32,16},{48,32},{64,48},{80,64},{96,80},{112,96},{128,112},... | collective-permute-start | bytes 393224 | tf_op jit(solution)/shard_map/while/body/eval_jaxpr/ppermute | solution.py:17
  579.9 8.4 %collective-permute-start.1 = (f32[1,2,128,128]{3,2,1,0:T(8,128)S(1)}, f32[1,2,128,128]{3,2,1,0:T(8,128)S(1)}, u32[]{:S(2)}, u32[]{:S(2)}) collective-permute-start(f32[1,2,128,128]{3,2,1,0:T(8,128)S(1)} %fusion.354), channel_id=1, source_target_pairs={{16,0},{32,16},{48,32},{64,48},{80,64},{96,80},{112,96},{128,112},... | collective-permute-start | bytes 393224 | tf_op jit(solution)/shard_map/while/body/eval_jaxpr/ppermute | solution.py:17
  588.6 8.4 %collective-permute-start.1 = (f32[1,2,128,128]{3,2,1,0:T(8,128)S(1)}, f32[1,2,128,128]{3,2,1,0:T(8,128)S(1)}, u32[]{:S(2)}, u32[]{:S(2)}) collective-permute-start(f32[1,2,128,128]{3,2,1,0:T(8,128)S(1)} %fusion.354), channel_id=1, source_target_pairs={{16,0},{32,16},{48,32},{64,48},{80,64},{96,80},{112,96},{128,112},... | collective-permute-start | bytes 393224 | tf_op jit(solution)/shard_map/while/body/eval_jaxpr/ppermute | solution.py:17
  597.2 8.4 %collective-permute-start.1 = (f32[1,2,128,128]{3,2,1,0:T(8,128)S(1)}, f32[1,2,128,128]{3,2,1,0:T(8,128)S(1)}, u32[]{:S(2)}, u32[]{:S(2)}) collective-permute-start(f32[1,2,128,128]{3,2,1,0:T(8,128)S(1)} %fusion.354), channel_id=1, source_target_pairs={{16,0},{32,16},{48,32},{64,48},{80,64},{96,80},{112,96},{128,112},... | collective-permute-start | bytes 393224 | tf_op jit(solution)/shard_map/while/body/eval_jaxpr/ppermute | solution.py:17
  605.9 8.4 %collective-permute-start.1 = (f32[1,2,128,128]{3,2,1,0:T(8,128)S(1)}, f32[1,2,128,128]{3,2,1,0:T(8,128)S(1)}, u32[]{:S(2)}, u32[]{:S(2)}) collective-permute-start(f32[1,2,128,128]{3,2,1,0:T(8,128)S(1)} %fusion.354), channel_id=1, source_target_pairs={{16,0},{32,16},{48,32},{64,48},{80,64},{96,80},{112,96},{128,112},... | collective-permute-start | bytes 393224 | tf_op jit(solution)/shard_map/while/body/eval_jaxpr/ppermute | solution.py:17
  614.6 8.4 %collective-permute-start.1 = (f32[1,2,128,128]{3,2,1,0:T(8,128)S(1)}, f32[1,2,128,128]{3,2,1,0:T(8,128)S(1)}, u32[]{:S(2)}, u32[]{:S(2)}) collective-permute-start(f32[1,2,128,128]{3,2,1,0:T(8,128)S(1)} %fusion.354), channel_id=1, source_target_pairs={{16,0},{32,16},{48,32},{64,48},{80,64},{96,80},{112,96},{128,112},... | collective-permute-start | bytes 393224 | tf_op jit(solution)/shard_map/while/body/eval_jaxpr/ppermute | solution.py:17
  623.2 8.4 %collective-permute-start.1 = (f32[1,2,128,128]{3,2,1,0:T(8,128)S(1)}, f32[1,2,128,128]{3,2,1,0:T(8,128)S(1)}, u32[]{:S(2)}, u32[]{:S(2)}) collective-permute-start(f32[1,2,128,128]{3,2,1,0:T(8,128)S(1)} %fusion.354), channel_id=1, source_target_pairs={{16,0},{32,16},{48,32},{64,48},{80,64},{96,80},{112,96},{128,112},... | collective-permute-start | bytes 393224 | tf_op jit(solution)/shard_map/while/body/eval_jaxpr/ppermute | solution.py:17
  631.9 8.4 %collective-permute-start.1 = (f32[1,2,128,128]{3,2,1,0:T(8,128)S(1)}, f32[1,2,128,128]{3,2,1,0:T(8,128)S(1)}, u32[]{:S(2)}, u32[]{:S(2)}) collective-permute-start(f32[1,2,128,128]{3,2,1,0:T(8,128)S(1)} %fusion.354), channel_id=1, source_target_pairs={{16,0},{32,16},{48,32},{64,48},{80,64},{96,80},{112,96},{128,112},... | collective-permute-start | bytes 393224 | tf_op jit(solution)/shard_map/while/body/eval_jaxpr/ppermute | solution.py:17
  640.6 8.4 %collective-permute-start.1 = (f32[1,2,128,128]{3,2,1,0:T(8,128)S(1)}, f32[1,2,128,128]{3,2,1,0:T(8,128)S(1)}, u32[]{:S(2)}, u32[]{:S(2)}) collective-permute-start(f32[1,2,128,128]{3,2,1,0:T(8,128)S(1)} %fusion.354), channel_id=1, source_target_pairs={{16,0},{32,16},{48,32},{64,48},{80,64},{96,80},{112,96},{128,112},... | collective-permute-start | bytes 393224 | tf_op jit(solution)/shard_map/while/body/eval_jaxpr/ppermute | solution.py:17
  649.3 8.4 %collective-permute-start.1 = (f32[1,2,128,128]{3,2,1,0:T(8,128)S(1)}, f32[1,2,128,128]{3,2,1,0:T(8,128)S(1)}, u32[]{:S(2)}, u32[]{:S(2)}) collective-permute-start(f32[1,2,128,128]{3,2,1,0:T(8,128)S(1)} %fusion.354), channel_id=1, source_target_pairs={{16,0},{32,16},{48,32},{64,48},{80,64},{96,80},{112,96},{128,112},... | collective-permute-start | bytes 393224 | tf_op jit(solution)/shard_map/while/body/eval_jaxpr/ppermute | solution.py:17
  657.9 8.4 %collective-permute-start.1 = (f32[1,2,128,128]{3,2,1,0:T(8,128)S(1)}, f32[1,2,128,128]{3,2,1,0:T(8,128)S(1)}, u32[]{:S(2)}, u32[]{:S(2)}) collective-permute-start(f32[1,2,128,128]{3,2,1,0:T(8,128)S(1)} %fusion.354), channel_id=1, source_target_pairs={{16,0},{32,16},{48,32},{64,48},{80,64},{96,80},{112,96},{128,112},... | collective-permute-start | bytes 393224 | tf_op jit(solution)/shard_map/while/body/eval_jaxpr/ppermute | solution.py:17
  (3 other events, 81.3 us)
Sparse Core Ops, SparseCore 0:
  363.8 101.0 reduce-scatter.1
where the time goes:
time: 709 us; the launch traced here: 706 us
  waiting for transfers between devices  266 us (38%)
  starting transfers between devices  259 us (37%)
  other arithmetic  89.1 us (13%)
  matrix products  38.5 us (5%)
  blocking collectives  32.1 us (5%)
  between operations  14.4 us (2%)
    ppermute x62, waiting for transfers between devices, from_behind(): lax.ppermute(value, axis, [(source, source + steps) for source in range(i...  266 us
    ppermute x62, starting transfers between devices, from_behind(): lax.ppermute(value, axis, [(source, source + steps) for source in range(i...  258 us
    another operation x16, other arithmetic, span_advance(): lax.linalg.triangular_solve(lower_mix, right_side, left_side=True, lower=...  39.9 us
    all_gather x1, blocking collectives, per_device(): full_grad = lax.all_gather(out_grad, 'head', axis=1, tiled=True)  32.1 us
    another operation x10, other arithmetic, retreat(): lax.linalg.triangular_solve(lower_mix, decay_cum[:, None] * key_block, le...  20 us
    another operation x8, other arithmetic, single_advance(): lax.linalg.triangular_solve(lower_mix, stacked, left_side=True, lower=Tru...  19.9 us
    dot_general x62, matrix products, matmul_states(): return jnp.einsum('abij,abjk->abik', left, right, precision=highest)  16.5 us
  transfers between devices with their start and end apart: 63, of which 62 were waited for; matrix products, arithmetic and copies ran while one was open for 9% of the time, Pallas kernels for 0%

commit v1 on v0

--- a/solution.py
+++ b/solution.py
@@ -223,7 +223,9 @@
         .transpose(1, 2, 0)
     )
     transition, local_state = jax.vmap(slab_effect)(key_heads, value_heads, decay_logs, betas)
-    full_grad = lax.all_gather(out_grad, "head", axis=1, tiled=True)
+    full_grad = jnp.concatenate(
+        lax.all_to_all(jnp.stack([out_grad] * lax.axis_size("head")), "head", 0, 0), axis=1
+    )
     out_cot = jnp.dot(full_grad, w_out.T, preferred_element_type=jnp.float32)
     cot_heads = out_cot.reshape(length, key_count, group, width).transpose(1, 2, 0, 3)
     empty_states = jnp.zeros_like(transition)

time: 709 us -> 771 us (1.087)
  the two profiles are of different devices: /device:TPU:15 before, /device:TPU:2 now
where the time goes in v1:
time: 771 us; the launch traced here: 769 us
  waiting for transfers between devices  362 us (47%)
  starting transfers between devices  242 us (31%)
  other arithmetic  93.4 us (12%)
  matrix products  38.4 us (5%)
  local copies, waits for them, and re-layouts  15.9 us (2%)
  between operations  14.6 us (2%)
    ppermute x62, waiting for transfers between devices, from_behind(): lax.ppermute(value, axis, [(source, source + steps) for source in range(i...  269 us
    ppermute x62, starting transfers between devices, from_behind(): lax.ppermute(value, axis, [(source, source + steps) for source in range(i...  227 us
    reduce_scatter x1, waiting for transfers between devices, per_device(): lax.psum_scatter(jnp.dot(attn_out.T, full_grad, preferred_element_type=jn...  92.9 us
    another operation x16, other arithmetic, span_advance(): lax.linalg.triangular_solve(lower_mix, right_side, left_side=True, lower=...  39.9 us
    another operation x10, other arithmetic, retreat(): lax.linalg.triangular_solve(lower_mix, decay_cum[:, None] * key_block, le...  20 us
    another operation x8, other arithmetic, single_advance(): lax.linalg.triangular_solve(lower_mix, stacked, left_side=True, lower=Tru...  19.9 us
    dot_general x62, matrix products, matmul_states(): return jnp.einsum('abij,abjk->abik', left, right, precision=highest)  16.5 us
  transfers between devices with their start and end apart: 64, of which 63 were waited for; matrix products, arithmetic and copies ran while one was open for 13% of the time, Pallas kernels for 0%

profile of v1, /device:TPU:2, one launch (start us, length us, event | category | flops | bytes accessed | tf_op | source)
XLA Modules:
  0.0 768.6 jit_solution(9010888730701171068)
XLA Ops:
  8.9 15.2 %all-to-all-start = ((bf16[16,128,128]{2,1,0:T(8,128)(2,1)}), bf16[16,128,128]{2,1,0:T(8,128)(2,1)S(1)}, u32[]{:S(2)}, u32[]{:S(2)}) async-start(bf16[16,128,128]{2,1,0:T(8,128)(2,1)} %stack.2), calls=%async_computation | async-start | bytes 1048576 | tf_op jit(solution)/shard_map/all_to_all | solution.py:227
  29.3 25.9 %while.114 = (s32[]{:T(128)}, f32[1,2,128,128]{3,2,1,0:T(8,128)S(1)}, f32[1,2,128,128]{3,2,1,0:T(8,128)S(1)}, f32[2,1,2,64]{3,2,1,0:T(2,128)S(1)}, f32[2,1,64,12...) while((s32[]{:T(128)}, ...), condition=%wide.region_3.4_spmd.clone, body=%wide.region_1.3_spmd.clone.sunk | while | flops 132489408 | bytes 2056892 | solution.py:120
  30.3 9.8 %custom-call.41 = f32[1,2,1,64,64]{3,4,2,1,0:T(8,128)S(1)} custom-call(f32[1,2,1,64,64]{4,3,2,1,0:T(8,128)S(1)} %select_add_fusion.2), custom_call_target="InvertDiagBlocksLowerTriangular" | custom-call | tf_op jit(solution)/shard_map/vmap(vmap())/while/body/eval_jaxpr/triangular_solve | solution.py:100
  43.2 9.8 %custom-call.41 = f32[1,2,1,64,64]{3,4,2,1,0:T(8,128)S(1)} custom-call(f32[1,2,1,64,64]{4,3,2,1,0:T(8,128)S(1)} %select_add_fusion.2), custom_call_target="InvertDiagBlocksLowerTriangular" | custom-call | tf_op jit(solution)/shard_map/vmap(vmap())/while/body/eval_jaxpr/triangular_solve | solution.py:100
  55.9 243.1 %while.110 = (s32[]{:T(128)}, f32[1,2,128,128]{3,2,1,0:T(8,128)S(1)}, f32[1,2,128,128]{3,2,1,0:T(8,128)S(1)}, f32[1,2,128,128]{3,2,1,0:T(8,128)S(1)}, s32[]{:T(128)}) while((s32[]{:T(128)}, f32[1,2,128,128]{3,2,1,0:T(8,128)S(1)}, f32[1,2,128,128]{3,2,1,0:T(8,128)S(1)}, f32[1,2,128,128]{3,2,1,0:T(8,128)S(1)}, s32[]{:T(128)}) %tuple.224), condition=%wide.region_5.6_spmd, body=%wide.region_4.5_spmd.sunk | while | flops 50364416 | bytes 1048677 | solution.py:239
  134.9 7.1 collective-permute-start
  143.2 7.4 collective-permute-start
  151.9 7.4 collective-permute-start
  160.6 7.4 collective-permute-start
  169.2 7.4 collective-permute-start
  177.9 7.4 collective-permute-start
  186.6 7.4 collective-permute-start
  195.2 7.4 collective-permute-start
  203.9 7.4 collective-permute-start
  212.6 7.4 collective-permute-start
  221.3 7.4 collective-permute-start
  229.9 7.4 collective-permute-start
  238.6 7.4 collective-permute-start
  247.3 7.4 collective-permute-start
  255.9 7.4 collective-permute-start
  264.6 7.4 collective-permute-start
  273.3 7.4 collective-permute-start
  281.9 7.4 collective-permute-start
  290.6 7.4 collective-permute-start
  299.0 30.5 %while.113 = (s32[]{:T(128)}, f32[1,2,128,128]{3,2,1,0:T(8,128)S(1)}, bf16[2,1,2,64,128]{4,3,0,2,1:T(8,128)(2,1)S(1)}, f32[2,1,128,64]{2,3,1,0:T(8,128)S(1)}, f3...) while((s32[]{:T(128)}, ...), condition=%wide.region_9.11_spmd.clone.clone, body=%wide.region_7.10_spmd.clone.clone.sunk | while | flops 113562048 | bytes 2288957 | solution.py:57
  301.2 9.8 %custom-call.40 = f32[1,2,1,64,64]{3,4,2,1,0:T(8,128)S(1)} custom-call(f32[1,2,1,64,64]{4,3,2,1,0:T(8,128)S(1)} %add_bitcast_fusion.7), custom_call_target="InvertDiagBlocksLowerTriangular" | custom-call | tf_op jit(solution)/shard_map/vmap(jvp(vmap()))/while/body/eval_jaxpr/triangular_solve/custom-call.0 | solution.py:45
  316.4 9.8 %custom-call.40 = f32[1,2,1,64,64]{3,4,2,1,0:T(8,128)S(1)} custom-call(f32[1,2,1,64,64]{4,3,2,1,0:T(8,128)S(1)} %add_bitcast_fusion.7), custom_call_target="InvertDiagBlocksLowerTriangular" | custom-call | tf_op jit(solution)/shard_map/vmap(jvp(vmap()))/while/body/eval_jaxpr/triangular_solve/custom-call.0 | solution.py:45
  335.4 28.4 %while.115 = (s32[]{:T(128)}, f32[1,2,128,128]{3,2,1,0:T(8,128)S(1)}, f32[2,1,2,64]{3,2,1,0:T(2,128)}, f32[2,1,64,128]{3,2,1,0:T(8,128)S(1)}, f32[2,1,2,64]{3,2,...) while((s32[]{:T(128)}, ...), condition=%wide.region_12.14_spmd.clone, body=%wide.region_10.13_spmd.clone.sunk | while | flops 113586368 | bytes 1705664 | solution.py:173
  337.7 9.8 %custom-call.42 = f32[1,2,1,64,64]{3,4,2,1,0:T(8,128)S(1)} custom-call(f32[1,2,1,64,64]{4,3,2,1,0:T(8,128)S(1)} %add_bitcast_fusion.8), custom_call_target="InvertDiagBlocksLowerTriangular" | custom-call | tf_op jit(solution)/shard_map/vmap(vmap())/while/body/eval_jaxpr/triangular_solve/custom-call.0 | solution.py:153
  351.9 9.8 %custom-call.42 = f32[1,2,1,64,64]{3,4,2,1,0:T(8,128)S(1)} custom-call(f32[1,2,1,64,64]{4,3,2,1,0:T(8,128)S(1)} %add_bitcast_fusion.8), custom_call_target="InvertDiagBlocksLowerTriangular" | custom-call | tf_op jit(solution)/shard_map/vmap(vmap())/while/body/eval_jaxpr/triangular_solve/custom-call.0 | solution.py:153
  363.9 270.5 %while.111 = (s32[]{:T(128)}, f32[1,2,128,128]{3,2,1,0:T(8,128)S(1)}, f32[1,2,128,128]{3,2,1,0:T(8,128)S(1)}, f32[1,2,128,128]{3,2,1,0:T(8,128)S(1)}, s32[]{:T(128)}) while((s32[]{:T(128)}, f32[1,2,128,128]{3,2,1,0:T(8,128)S(1)}, f32[1,2,128,128]{3,2,1,0:T(8,128)S(1)}, f32[1,2,128,128]{3,2,1,0:T(8,128)S(1)}, s32[]{:T(128)}) %tuple.233), condition=%wide.region_14.16_spmd, body=%wide.region_13.15_spmd.sunk | while | flops 50364416 | bytes 1048677 | solution.py:244
  366.1 6.3 collective-permute-done.1
  374.6 7.2 collective-permute-done.1
  392.5 7.2 collective-permute-done.1
  410.5 7.2 collective-permute-done.1
  419.8 6.5 collective-permute-done.1
  428.5 6.5 collective-permute-done.1
  437.2 6.5 collective-permute-done.1
  445.9 6.5 collective-permute-done.1
  454.5 6.5 collective-permute-done.1
  463.2 6.5 collective-permute-done.1
  471.9 6.5 collective-permute-done.1
  480.5 6.5 collective-permute-done.1
  489.2 6.5 collective-permute-done.1
  497.9 6.5 collective-permute-done.1
  506.5 6.5 collective-permute-done.1
  515.2 6.5 collective-permute-done.1
  523.9 6.5 collective-permute-done.1
  532.6 6.5 collective-permute-done.1
  541.2 6.5 collective-permute-done.1
  549.9 6.5 collective-permute-done.1
  558.6 6.5 collective-permute-done.1
  567.2 6.5 collective-permute-done.1
  575.9 6.5 collective-permute-done.1
  584.6 6.5 collective-permute-done.1
  593.3 6.5 collective-permute-done.1
  601.9 6.5 collective-permute-done.1
  610.6 6.5 collective-permute-done.1
  619.3 6.5 collective-permute-done.1
  627.9 6.5 collective-permute-done.1
  636.5 28.2 %while.112 = (s32[]{:T(128)}, f32[1,2,128,128]{2,3,1,0:T(8,128)S(1)}, f32[2,1,64,128]{3,2,1,0:T(8,128)S(1)}, f32[2,1,64,128]{3,2,1,0:T(8,128)S(1)}, f32[2,1,2,64...) while((s32[]{:T(128)}, ...), condition=%wide.region_18.20_spmd.clone, body=%wide.region_15.19_spmd.clone.sunk | while | flops 233140288 | bytes 3349265 | solution.py:57
  637.2 9.8 %custom-call.39 = f32[1,2,1,64,64]{3,4,2,1,0:T(8,128)S(1)} custom-call(f32[1,2,1,64,64]{4,3,2,1,0:T(8,128)S(1)} %add_bitcast_fusion.6), custom_call_target="InvertDiagBlocksLowerTriangular" | custom-call | tf_op jit(solution)/shard_map/vmap(transpose(jvp(vmap())))/while/body/eval_jaxpr/triangular_solve | solution.py:45
  651.3 9.8 %custom-call.39 = f32[1,2,1,64,64]{3,4,2,1,0:T(8,128)S(1)} custom-call(f32[1,2,1,64,64]{4,3,2,1,0:T(8,128)S(1)} %add_bitcast_fusion.6), custom_call_target="InvertDiagBlocksLowerTriangular" | custom-call | tf_op jit(solution)/shard_map/vmap(transpose(jvp(vmap())))/while/body/eval_jaxpr/triangular_solve | solution.py:45
  667.3 92.9 %reduce-scatter.2.cloned.1.call-done = f32[8,2048]{1,0:T(8,128)} async-done(((f32[256,2048]{1,0:T(8,128)}), f32[8,2048]{1,0:T(8,128)}) %reduce-scatter.2.cloned.1.call-update) | async-done | bytes 65552 | tf_op jit(solution)/shard_map/reduce_scatter | solution.py:258
  (399 shorter events, 234.9 us)
Async XLA Ops:
  8.9 323.6 %all-to-all-start = ((bf16[16,128,128]{2,1,0:T(8,128)(2,1)}), bf16[16,128,128]{2,1,0:T(8,128)(2,1)S(1)}, u32[]{:S(2)}, u32[]{:S(2)}) async-start(bf16[16,128,128]{2,1,0:T(8,128)(2,1)} %stack.2), calls=%async_computation | async-start | bytes 1048576 | tf_op jit(solution)/shard_map/all_to_all | solution.py:227
  24.1 736.1 %reduce-scatter.2.cloned.1.call-start = ((), (), s32[]{:S(2)}) async-start(), calls=%async_computation.2 | async-start | bytes 2162688 | tf_op jit(solution)/shard_map/reduce_scatter | solution.py:258
  56.2 6.3 collective-permute-start
  62.7 6.3 collective-permute-start
  69.3 6.3 collective-permute-start
  75.9 6.3 collective-permute-start
  82.4 6.3 collective-permute-start
  89.0 6.3 collective-permute-start
  95.5 6.3 collective-permute-start
  102.1 6.3 collective-permute-start
  108.7 6.3 collective-permute-start
  115.2 6.3 collective-permute-start
  121.8 6.3 collective-permute-start
  128.4 6.3 collective-permute-start
  134.9 8.0 %collective-permute-start = (f32[1,2,128,128]{3,2,1,0:T(8,128)S(1)}, f32[1,2,128,128]{3,2,1,0:T(8,128)S(1)}, u32[]{:S(2)}, u32[]{:S(2)}) collective-permute-start(f32[1,2,128,128]{3,2,1,0:T(8,128)S(1)} %fusion.353), channel_id=1, source_target_pairs={{0,16},{16,32},{32,48},{48,64},{64,80},{80,96},{96,112},{112,128},... | collective-permute-start | bytes 393224 | tf_op jit(solution)/shard_map/while/body/eval_jaxpr/ppermute | solution.py:17
  143.2 8.4 %collective-permute-start = (f32[1,2,128,128]{3,2,1,0:T(8,128)S(1)}, f32[1,2,128,128]{3,2,1,0:T(8,128)S(1)}, u32[]{:S(2)}, u32[]{:S(2)}) collective-permute-start(f32[1,2,128,128]{3,2,1,0:T(8,128)S(1)} %fusion.353), channel_id=1, source_target_pairs={{0,16},{16,32},{32,48},{48,64},{64,80},{80,96},{96,112},{112,128},... | collective-permute-start | bytes 393224 | tf_op jit(solution)/shard_map/while/body/eval_jaxpr/ppermute | solution.py:17
  151.9 8.4 %collective-permute-start = (f32[1,2,128,128]{3,2,1,0:T(8,128)S(1)}, f32[1,2,128,128]{3,2,1,0:T(8,128)S(1)}, u32[]{:S(2)}, u32[]{:S(2)}) collective-permute-start(f32[1,2,128,128]{3,2,1,0:T(8,128)S(1)} %fusion.353), channel_id=1, source_target_pairs={{0,16},{16,32},{32,48},{48,64},{64,80},{80,96},{96,112},{112,128},... | collective-permute-start | bytes 393224 | tf_op jit(solution)/shard_map/while/body/eval_jaxpr/ppermute | solution.py:17
  160.6 8.4 %collective-permute-start = (f32[1,2,128,128]{3,2,1,0:T(8,128)S(1)}, f32[1,2,128,128]{3,2,1,0:T(8,128)S(1)}, u32[]{:S(2)}, u32[]{:S(2)}) collective-permute-start(f32[1,2,128,128]{3,2,1,0:T(8,128)S(1)} %fusion.353), channel_id=1, source_target_pairs={{0,16},{16,32},{32,48},{48,64},{64,80},{80,96},{96,112},{112,128},... | collective-permute-start | bytes 393224 | tf_op jit(solution)/shard_map/while/body/eval_jaxpr/ppermute | solution.py:17
  169.2 8.4 %collective-permute-start = (f32[1,2,128,128]{3,2,1,0:T(8,128)S(1)}, f32[1,2,128,128]{3,2,1,0:T(8,128)S(1)}, u32[]{:S(2)}, u32[]{:S(2)}) collective-permute-start(f32[1,2,128,128]{3,2,1,0:T(8,128)S(1)} %fusion.353), channel_id=1, source_target_pairs={{0,16},{16,32},{32,48},{48,64},{64,80},{80,96},{96,112},{112,128},... | collective-permute-start | bytes 393224 | tf_op jit(solution)/shard_map/while/body/eval_jaxpr/ppermute | solution.py:17
  177.9 8.4 %collective-permute-start = (f32[1,2,128,128]{3,2,1,0:T(8,128)S(1)}, f32[1,2,128,128]{3,2,1,0:T(8,128)S(1)}, u32[]{:S(2)}, u32[]{:S(2)}) collective-permute-start(f32[1,2,128,128]{3,2,1,0:T(8,128)S(1)} %fusion.353), channel_id=1, source_target_pairs={{0,16},{16,32},{32,48},{48,64},{64,80},{80,96},{96,112},{112,128},... | collective-permute-start | bytes 393224 | tf_op jit(solution)/shard_map/while/body/eval_jaxpr/ppermute | solution.py:17
  186.6 8.4 %collective-permute-start = (f32[1,2,128,128]{3,2,1,0:T(8,128)S(1)}, f32[1,2,128,128]{3,2,1,0:T(8,128)S(1)}, u32[]{:S(2)}, u32[]{:S(2)}) collective-permute-start(f32[1,2,128,128]{3,2,1,0:T(8,128)S(1)} %fusion.353), channel_id=1, source_target_pairs={{0,16},{16,32},{32,48},{48,64},{64,80},{80,96},{96,112},{112,128},... | collective-permute-start | bytes 393224 | tf_op jit(solution)/shard_map/while/body/eval_jaxpr/ppermute | solution.py:17
  195.2 8.4 %collective-permute-start = (f32[1,2,128,128]{3,2,1,0:T(8,128)S(1)}, f32[1,2,128,128]{3,2,1,0:T(8,128)S(1)}, u32[]{:S(2)}, u32[]{:S(2)}) collective-permute-start(f32[1,2,128,128]{3,2,1,0:T(8,128)S(1)} %fusion.353), channel_id=1, source_target_pairs={{0,16},{16,32},{32,48},{48,64},{64,80},{80,96},{96,112},{112,128},... | collective-permute-start | bytes 393224 | tf_op jit(solution)/shard_map/while/body/eval_jaxpr/ppermute | solution.py:17
  203.9 8.4 %collective-permute-start = (f32[1,2,128,128]{3,2,1,0:T(8,128)S(1)}, f32[1,2,128,128]{3,2,1,0:T(8,128)S(1)}, u32[]{:S(2)}, u32[]{:S(2)}) collective-permute-start(f32[1,2,128,128]{3,2,1,0:T(8,128)S(1)} %fusion.353), channel_id=1, source_target_pairs={{0,16},{16,32},{32,48},{48,64},{64,80},{80,96},{96,112},{112,128},... | collective-permute-start | bytes 393224 | tf_op jit(solution)/shard_map/while/body/eval_jaxpr/ppermute | solution.py:17
  212.6 8.4 %collective-permute-start = (f32[1,2,128,128]{3,2,1,0:T(8,128)S(1)}, f32[1,2,128,128]{3,2,1,0:T(8,128)S(1)}, u32[]{:S(2)}, u32[]{:S(2)}) collective-permute-start(f32[1,2,128,128]{3,2,1,0:T(8,128)S(1)} %fusion.353), channel_id=1, source_target_pairs={{0,16},{16,32},{32,48},{48,64},{64,80},{80,96},{96,112},{112,128},... | collective-permute-start | bytes 393224 | tf_op jit(solution)/shard_map/while/body/eval_jaxpr/ppermute | solution.py:17
  221.3 8.4 %collective-permute-start = (f32[1,2,128,128]{3,2,1,0:T(8,128)S(1)}, f32[1,2,128,128]{3,2,1,0:T(8,128)S(1)}, u32[]{:S(2)}, u32[]{:S(2)}) collective-permute-start(f32[1,2,128,128]{3,2,1,0:T(8,128)S(1)} %fusion.353), channel_id=1, source_target_pairs={{0,16},{16,32},{32,48},{48,64},{64,80},{80,96},{96,112},{112,128},... | collective-permute-start | bytes 393224 | tf_op jit(solution)/shard_map/while/body/eval_jaxpr/ppermute | solution.py:17
  229.9 8.4 %collective-permute-start = (f32[1,2,128,128]{3,2,1,0:T(8,128)S(1)}, f32[1,2,128,128]{3,2,1,0:T(8,128)S(1)}, u32[]{:S(2)}, u32[]{:S(2)}) collective-permute-start(f32[1,2,128,128]{3,2,1,0:T(8,128)S(1)} %fusion.353), channel_id=1, source_target_pairs={{0,16},{16,32},{32,48},{48,64},{64,80},{80,96},{96,112},{112,128},... | collective-permute-start | bytes 393224 | tf_op jit(solution)/shard_map/while/body/eval_jaxpr/ppermute | solution.py:17
  238.6 8.4 %collective-permute-start = (f32[1,2,128,128]{3,2,1,0:T(8,128)S(1)}, f32[1,2,128,128]{3,2,1,0:T(8,128)S(1)}, u32[]{:S(2)}, u32[]{:S(2)}) collective-permute-start(f32[1,2,128,128]{3,2,1,0:T(8,128)S(1)} %fusion.353), channel_id=1, source_target_pairs={{0,16},{16,32},{32,48},{48,64},{64,80},{80,96},{96,112},{112,128},... | collective-permute-start | bytes 393224 | tf_op jit(solution)/shard_map/while/body/eval_jaxpr/ppermute | solution.py:17
  247.3 8.4 %collective-permute-start = (f32[1,2,128,128]{3,2,1,0:T(8,128)S(1)}, f32[1,2,128,128]{3,2,1,0:T(8,128)S(1)}, u32[]{:S(2)}, u32[]{:S(2)}) collective-permute-start(f32[1,2,128,128]{3,2,1,0:T(8,128)S(1)} %fusion.353), channel_id=1, source_target_pairs={{0,16},{16,32},{32,48},{48,64},{64,80},{80,96},{96,112},{112,128},... | collective-permute-start | bytes 393224 | tf_op jit(solution)/shard_map/while/body/eval_jaxpr/ppermute | solution.py:17
  255.9 8.4 %collective-permute-start = (f32[1,2,128,128]{3,2,1,0:T(8,128)S(1)}, f32[1,2,128,128]{3,2,1,0:T(8,128)S(1)}, u32[]{:S(2)}, u32[]{:S(2)}) collective-permute-start(f32[1,2,128,128]{3,2,1,0:T(8,128)S(1)} %fusion.353), channel_id=1, source_target_pairs={{0,16},{16,32},{32,48},{48,64},{64,80},{80,96},{96,112},{112,128},... | collective-permute-start | bytes 393224 | tf_op jit(solution)/shard_map/while/body/eval_jaxpr/ppermute | solution.py:17
  264.6 8.4 %collective-permute-start = (f32[1,2,128,128]{3,2,1,0:T(8,128)S(1)}, f32[1,2,128,128]{3,2,1,0:T(8,128)S(1)}, u32[]{:S(2)}, u32[]{:S(2)}) collective-permute-start(f32[1,2,128,128]{3,2,1,0:T(8,128)S(1)} %fusion.353), channel_id=1, source_target_pairs={{0,16},{16,32},{32,48},{48,64},{64,80},{80,96},{96,112},{112,128},... | collective-permute-start | bytes 393224 | tf_op jit(solution)/shard_map/while/body/eval_jaxpr/ppermute | solution.py:17
  273.3 8.4 %collective-permute-start = (f32[1,2,128,128]{3,2,1,0:T(8,128)S(1)}, f32[1,2,128,128]{3,2,1,0:T(8,128)S(1)}, u32[]{:S(2)}, u32[]{:S(2)}) collective-permute-start(f32[1,2,128,128]{3,2,1,0:T(8,128)S(1)} %fusion.353), channel_id=1, source_target_pairs={{0,16},{16,32},{32,48},{48,64},{64,80},{80,96},{96,112},{112,128},... | collective-permute-start | bytes 393224 | tf_op jit(solution)/shard_map/while/body/eval_jaxpr/ppermute | solution.py:17
  281.9 8.4 %collective-permute-start = (f32[1,2,128,128]{3,2,1,0:T(8,128)S(1)}, f32[1,2,128,128]{3,2,1,0:T(8,128)S(1)}, u32[]{:S(2)}, u32[]{:S(2)}) collective-permute-start(f32[1,2,128,128]{3,2,1,0:T(8,128)S(1)} %fusion.353), channel_id=1, source_target_pairs={{0,16},{16,32},{32,48},{48,64},{64,80},{80,96},{96,112},{112,128},... | collective-permute-start | bytes 393224 | tf_op jit(solution)/shard_map/while/body/eval_jaxpr/ppermute | solution.py:17
  290.6 8.4 %collective-permute-start = (f32[1,2,128,128]{3,2,1,0:T(8,128)S(1)}, f32[1,2,128,128]{3,2,1,0:T(8,128)S(1)}, u32[]{:S(2)}, u32[]{:S(2)}) collective-permute-start(f32[1,2,128,128]{3,2,1,0:T(8,128)S(1)} %fusion.353), channel_id=1, source_target_pairs={{0,16},{16,32},{32,48},{48,64},{64,80},{80,96},{96,112},{112,128},... | collective-permute-start | bytes 393224 | tf_op jit(solution)/shard_map/while/body/eval_jaxpr/ppermute | solution.py:17
  364.2 8.3 %collective-permute-start.1 = (f32[1,2,128,128]{3,2,1,0:T(8,128)S(1)}, f32[1,2,128,128]{3,2,1,0:T(8,128)S(1)}, u32[]{:S(2)}, u32[]{:S(2)}) collective-permute-start(f32[1,2,128,128]{3,2,1,0:T(8,128)S(1)} %fusion.356), channel_id=1, source_target_pairs={{16,0},{32,16},{48,32},{64,48},{80,64},{96,80},{112,96},{128,112},... | collective-permute-start | bytes 393224 | tf_op jit(solution)/shard_map/while/body/eval_jaxpr/ppermute | solution.py:17
  372.7 9.1 %collective-permute-start.1 = (f32[1,2,128,128]{3,2,1,0:T(8,128)S(1)}, f32[1,2,128,128]{3,2,1,0:T(8,128)S(1)}, u32[]{:S(2)}, u32[]{:S(2)}) collective-permute-start(f32[1,2,128,128]{3,2,1,0:T(8,128)S(1)} %fusion.356), channel_id=1, source_target_pairs={{16,0},{32,16},{48,32},{64,48},{80,64},{96,80},{112,96},{128,112},... | collective-permute-start | bytes 393224 | tf_op jit(solution)/shard_map/while/body/eval_jaxpr/ppermute | solution.py:17
  382.1 8.3 %collective-permute-start.1 = (f32[1,2,128,128]{3,2,1,0:T(8,128)S(1)}, f32[1,2,128,128]{3,2,1,0:T(8,128)S(1)}, u32[]{:S(2)}, u32[]{:S(2)}) collective-permute-start(f32[1,2,128,128]{3,2,1,0:T(8,128)S(1)} %fusion.356), channel_id=1, source_target_pairs={{16,0},{32,16},{48,32},{64,48},{80,64},{96,80},{112,96},{128,112},... | collective-permute-start | bytes 393224 | tf_op jit(solution)/shard_map/while/body/eval_jaxpr/ppermute | solution.py:17
  390.6 9.1 %collective-permute-start.1 = (f32[1,2,128,128]{3,2,1,0:T(8,128)S(1)}, f32[1,2,128,128]{3,2,1,0:T(8,128)S(1)}, u32[]{:S(2)}, u32[]{:S(2)}) collective-permute-start(f32[1,2,128,128]{3,2,1,0:T(8,128)S(1)} %fusion.356), channel_id=1, source_target_pairs={{16,0},{32,16},{48,32},{64,48},{80,64},{96,80},{112,96},{128,112},... | collective-permute-start | bytes 393224 | tf_op jit(solution)/shard_map/while/body/eval_jaxpr/ppermute | solution.py:17
  400.0 8.3 %collective-permute-start.1 = (f32[1,2,128,128]{3,2,1,0:T(8,128)S(1)}, f32[1,2,128,128]{3,2,1,0:T(8,128)S(1)}, u32[]{:S(2)}, u32[]{:S(2)}) collective-permute-start(f32[1,2,128,128]{3,2,1,0:T(8,128)S(1)} %fusion.356), channel_id=1, source_target_pairs={{16,0},{32,16},{48,32},{64,48},{80,64},{96,80},{112,96},{128,112},... | collective-permute-start | bytes 393224 | tf_op jit(solution)/shard_map/while/body/eval_jaxpr/ppermute | solution.py:17
  408.5 9.1 %collective-permute-start.1 = (f32[1,2,128,128]{3,2,1,0:T(8,128)S(1)}, f32[1,2,128,128]{3,2,1,0:T(8,128)S(1)}, u32[]{:S(2)}, u32[]{:S(2)}) collective-permute-start(f32[1,2,128,128]{3,2,1,0:T(8,128)S(1)} %fusion.356), channel_id=1, source_target_pairs={{16,0},{32,16},{48,32},{64,48},{80,64},{96,80},{112,96},{128,112},... | collective-permute-start | bytes 393224 | tf_op jit(solution)/shard_map/while/body/eval_jaxpr/ppermute | solution.py:17
  417.9 8.4 %collective-permute-start.1 = (f32[1,2,128,128]{3,2,1,0:T(8,128)S(1)}, f32[1,2,128,128]{3,2,1,0:T(8,128)S(1)}, u32[]{:S(2)}, u32[]{:S(2)}) collective-permute-start(f32[1,2,128,128]{3,2,1,0:T(8,128)S(1)} %fusion.356), channel_id=1, source_target_pairs={{16,0},{32,16},{48,32},{64,48},{80,64},{96,80},{112,96},{128,112},... | collective-permute-start | bytes 393224 | tf_op jit(solution)/shard_map/while/body/eval_jaxpr/ppermute | solution.py:17
  426.6 8.4 %collective-permute-start.1 = (f32[1,2,128,128]{3,2,1,0:T(8,128)S(1)}, f32[1,2,128,128]{3,2,1,0:T(8,128)S(1)}, u32[]{:S(2)}, u32[]{:S(2)}) collective-permute-start(f32[1,2,128,128]{3,2,1,0:T(8,128)S(1)} %fusion.356), channel_id=1, source_target_pairs={{16,0},{32,16},{48,32},{64,48},{80,64},{96,80},{112,96},{128,112},... | collective-permute-start | bytes 393224 | tf_op jit(solution)/shard_map/while/body/eval_jaxpr/ppermute | solution.py:17
  435.2 8.4 %collective-permute-start.1 = (f32[1,2,128,128]{3,2,1,0:T(8,128)S(1)}, f32[1,2,128,128]{3,2,1,0:T(8,128)S(1)}, u32[]{:S(2)}, u32[]{:S(2)}) collective-permute-start(f32[1,2,128,128]{3,2,1,0:T(8,128)S(1)} %fusion.356), channel_id=1, source_target_pairs={{16,0},{32,16},{48,32},{64,48},{80,64},{96,80},{112,96},{128,112},... | collective-permute-start | bytes 393224 | tf_op jit(solution)/shard_map/while/body/eval_jaxpr/ppermute | solution.py:17
  443.9 8.4 %collective-permute-start.1 = (f32[1,2,128,128]{3,2,1,0:T(8,128)S(1)}, f32[1,2,128,128]{3,2,1,0:T(8,128)S(1)}, u32[]{:S(2)}, u32[]{:S(2)}) collective-permute-start(f32[1,2,128,128]{3,2,1,0:T(8,128)S(1)} %fusion.356), channel_id=1, source_target_pairs={{16,0},{32,16},{48,32},{64,48},{80,64},{96,80},{112,96},{128,112},... | collective-permute-start | bytes 393224 | tf_op jit(solution)/shard_map/while/body/eval_jaxpr/ppermute | solution.py:17
  452.6 8.4 %collective-permute-start.1 = (f32[1,2,128,128]{3,2,1,0:T(8,128)S(1)}, f32[1,2,128,128]{3,2,1,0:T(8,128)S(1)}, u32[]{:S(2)}, u32[]{:S(2)}) collective-permute-start(f32[1,2,128,128]{3,2,1,0:T(8,128)S(1)} %fusion.356), channel_id=1, source_target_pairs={{16,0},{32,16},{48,32},{64,48},{80,64},{96,80},{112,96},{128,112},... | collective-permute-start | bytes 393224 | tf_op jit(solution)/shard_map/while/body/eval_jaxpr/ppermute | solution.py:17
  461.3 8.4 %collective-permute-start.1 = (f32[1,2,128,128]{3,2,1,0:T(8,128)S(1)}, f32[1,2,128,128]{3,2,1,0:T(8,128)S(1)}, u32[]{:S(2)}, u32[]{:S(2)}) collective-permute-start(f32[1,2,128,128]{3,2,1,0:T(8,128)S(1)} %fusion.356), channel_id=1, source_target_pairs={{16,0},{32,16},{48,32},{64,48},{80,64},{96,80},{112,96},{128,112},... | collective-permute-start | bytes 393224 | tf_op jit(solution)/shard_map/while/body/eval_jaxpr/ppermute | solution.py:17
  469.9 8.4 %collective-permute-start.1 = (f32[1,2,128,128]{3,2,1,0:T(8,128)S(1)}, f32[1,2,128,128]{3,2,1,0:T(8,128)S(1)}, u32[]{:S(2)}, u32[]{:S(2)}) collective-permute-start(f32[1,2,128,128]{3,2,1,0:T(8,128)S(1)} %fusion.356), channel_id=1, source_target_pairs={{16,0},{32,16},{48,32},{64,48},{80,64},{96,80},{112,96},{128,112},... | collective-permute-start | bytes 393224 | tf_op jit(solution)/shard_map/while/body/eval_jaxpr/ppermute | solution.py:17
  478.6 8.4 %collective-permute-start.1 = (f32[1,2,128,128]{3,2,1,0:T(8,128)S(1)}, f32[1,2,128,128]{3,2,1,0:T(8,128)S(1)}, u32[]{:S(2)}, u32[]{:S(2)}) collective-permute-start(f32[1,2,128,128]{3,2,1,0:T(8,128)S(1)} %fusion.356), channel_id=1, source_target_pairs={{16,0},{32,16},{48,32},{64,48},{80,64},{96,80},{112,96},{128,112},... | collective-permute-start | bytes 393224 | tf_op jit(solution)/shard_map/while/body/eval_jaxpr/ppermute | solution.py:17
  487.3 8.4 %collective-permute-start.1 = (f32[1,2,128,128]{3,2,1,0:T(8,128)S(1)}, f32[1,2,128,128]{3,2,1,0:T(8,128)S(1)}, u32[]{:S(2)}, u32[]{:S(2)}) collective-permute-start(f32[1,2,128,128]{3,2,1,0:T(8,128)S(1)} %fusion.356), channel_id=1, source_target_pairs={{16,0},{32,16},{48,32},{64,48},{80,64},{96,80},{112,96},{128,112},... | collective-permute-start | bytes 393224 | tf_op jit(solution)/shard_map/while/body/eval_jaxpr/ppermute | solution.py:17
  495.9 8.4 %collective-permute-start.1 = (f32[1,2,128,128]{3,2,1,0:T(8,128)S(1)}, f32[1,2,128,128]{3,2,1,0:T(8,128)S(1)}, u32[]{:S(2)}, u32[]{:S(2)}) collective-permute-start(f32[1,2,128,128]{3,2,1,0:T(8,128)S(1)} %fusion.356), channel_id=1, source_target_pairs={{16,0},{32,16},{48,32},{64,48},{80,64},{96,80},{112,96},{128,112},... | collective-permute-start | bytes 393224 | tf_op jit(solution)/shard_map/while/body/eval_jaxpr/ppermute | solution.py:17
  504.6 8.4 %collective-permute-start.1 = (f32[1,2,128,128]{3,2,1,0:T(8,128)S(1)}, f32[1,2,128,128]{3,2,1,0:T(8,128)S(1)}, u32[]{:S(2)}, u32[]{:S(2)}) collective-permute-start(f32[1,2,128,128]{3,2,1,0:T(8,128)S(1)} %fusion.356), channel_id=1, source_target_pairs={{16,0},{32,16},{48,32},{64,48},{80,64},{96,80},{112,96},{128,112},... | collective-permute-start | bytes 393224 | tf_op jit(solution)/shard_map/while/body/eval_jaxpr/ppermute | solution.py:17
  513.3 8.4 %collective-permute-start.1 = (f32[1,2,128,128]{3,2,1,0:T(8,128)S(1)}, f32[1,2,128,128]{3,2,1,0:T(8,128)S(1)}, u32[]{:S(2)}, u32[]{:S(2)}) collective-permute-start(f32[1,2,128,128]{3,2,1,0:T(8,128)S(1)} %fusion.356), channel_id=1, source_target_pairs={{16,0},{32,16},{48,32},{64,48},{80,64},{96,80},{112,96},{128,112},... | collective-permute-start | bytes 393224 | tf_op jit(solution)/shard_map/while/body/eval_jaxpr/ppermute | solution.py:17
  522.0 8.4 %collective-permute-start.1 = (f32[1,2,128,128]{3,2,1,0:T(8,128)S(1)}, f32[1,2,128,128]{3,2,1,0:T(8,128)S(1)}, u32[]{:S(2)}, u32[]{:S(2)}) collective-permute-start(f32[1,2,128,128]{3,2,1,0:T(8,128)S(1)} %fusion.356), channel_id=1, source_target_pairs={{16,0},{32,16},{48,32},{64,48},{80,64},{96,80},{112,96},{128,112},... | collective-permute-start | bytes 393224 | tf_op jit(solution)/shard_map/while/body/eval_jaxpr/ppermute | solution.py:17
  530.6 8.4 %collective-permute-start.1 = (f32[1,2,128,128]{3,2,1,0:T(8,128)S(1)}, f32[1,2,128,128]{3,2,1,0:T(8,128)S(1)}, u32[]{:S(2)}, u32[]{:S(2)}) collective-permute-start(f32[1,2,128,128]{3,2,1,0:T(8,128)S(1)} %fusion.356), channel_id=1, source_target_pairs={{16,0},{32,16},{48,32},{64,48},{80,64},{96,80},{112,96},{128,112},... | collective-permute-start | bytes 393224 | tf_op jit(solution)/shard_map/while/body/eval_jaxpr/ppermute | solution.py:17
  539.3 8.4 %collective-permute-start.1 = (f32[1,2,128,128]{3,2,1,0:T(8,128)S(1)}, f32[1,2,128,128]{3,2,1,0:T(8,128)S(1)}, u32[]{:S(2)}, u32[]{:S(2)}) collective-permute-start(f32[1,2,128,128]{3,2,1,0:T(8,128)S(1)} %fusion.356), channel_id=1, source_target_pairs={{16,0},{32,16},{48,32},{64,48},{80,64},{96,80},{112,96},{128,112},... | collective-permute-start | bytes 393224 | tf_op jit(solution)/shard_map/while/body/eval_jaxpr/ppermute | solution.py:17
  548.0 8.4 %collective-permute-start.1 = (f32[1,2,128,128]{3,2,1,0:T(8,128)S(1)}, f32[1,2,128,128]{3,2,1,0:T(8,128)S(1)}, u32[]{:S(2)}, u32[]{:S(2)}) collective-permute-start(f32[1,2,128,128]{3,2,1,0:T(8,128)S(1)} %fusion.356), channel_id=1, source_target_pairs={{16,0},{32,16},{48,32},{64,48},{80,64},{96,80},{112,96},{128,112},... | collective-permute-start | bytes 393224 | tf_op jit(solution)/shard_map/while/body/eval_jaxpr/ppermute | solution.py:17
  556.6 8.4 %collective-permute-start.1 = (f32[1,2,128,128]{3,2,1,0:T(8,128)S(1)}, f32[1,2,128,128]{3,2,1,0:T(8,128)S(1)}, u32[]{:S(2)}, u32[]{:S(2)}) collective-permute-start(f32[1,2,128,128]{3,2,1,0:T(8,128)S(1)} %fusion.356), channel_id=1, source_target_pairs={{16,0},{32,16},{48,32},{64,48},{80,64},{96,80},{112,96},{128,112},... | collective-permute-start | bytes 393224 | tf_op jit(solution)/shard_map/while/body/eval_jaxpr/ppermute | solution.py:17
  565.3 8.4 %collective-permute-start.1 = (f32[1,2,128,128]{3,2,1,0:T(8,128)S(1)}, f32[1,2,128,128]{3,2,1,0:T(8,128)S(1)}, u32[]{:S(2)}, u32[]{:S(2)}) collective-permute-start(f32[1,2,128,128]{3,2,1,0:T(8,128)S(1)} %fusion.356), channel_id=1, source_target_pairs={{16,0},{32,16},{48,32},{64,48},{80,64},{96,80},{112,96},{128,112},... | collective-permute-start | bytes 393224 | tf_op jit(solution)/shard_map/while/body/eval_jaxpr/ppermute | solution.py:17
  574.0 8.4 %collective-permute-start.1 = (f32[1,2,128,128]{3,2,1,0:T(8,128)S(1)}, f32[1,2,128,128]{3,2,1,0:T(8,128)S(1)}, u32[]{:S(2)}, u32[]{:S(2)}) collective-permute-start(f32[1,2,128,128]{3,2,1,0:T(8,128)S(1)} %fusion.356), channel_id=1, source_target_pairs={{16,0},{32,16},{48,32},{64,48},{80,64},{96,80},{112,96},{128,112},... | collective-permute-start | bytes 393224 | tf_op jit(solution)/shard_map/while/body/eval_jaxpr/ppermute | solution.py:17
  582.7 8.4 %collective-permute-start.1 = (f32[1,2,128,128]{3,2,1,0:T(8,128)S(1)}, f32[1,2,128,128]{3,2,1,0:T(8,128)S(1)}, u32[]{:S(2)}, u32[]{:S(2)}) collective-permute-start(f32[1,2,128,128]{3,2,1,0:T(8,128)S(1)} %fusion.356), channel_id=1, source_target_pairs={{16,0},{32,16},{48,32},{64,48},{80,64},{96,80},{112,96},{128,112},... | collective-permute-start | bytes 393224 | tf_op jit(solution)/shard_map/while/body/eval_jaxpr/ppermute | solution.py:17
  591.3 8.4 %collective-permute-start.1 = (f32[1,2,128,128]{3,2,1,0:T(8,128)S(1)}, f32[1,2,128,128]{3,2,1,0:T(8,128)S(1)}, u32[]{:S(2)}, u32[]{:S(2)}) collective-permute-start(f32[1,2,128,128]{3,2,1,0:T(8,128)S(1)} %fusion.356), channel_id=1, source_target_pairs={{16,0},{32,16},{48,32},{64,48},{80,64},{96,80},{112,96},{128,112},... | collective-permute-start | bytes 393224 | tf_op jit(solution)/shard_map/while/body/eval_jaxpr/ppermute | solution.py:17
  600.0 8.4 %collective-permute-start.1 = (f32[1,2,128,128]{3,2,1,0:T(8,128)S(1)}, f32[1,2,128,128]{3,2,1,0:T(8,128)S(1)}, u32[]{:S(2)}, u32[]{:S(2)}) collective-permute-start(f32[1,2,128,128]{3,2,1,0:T(8,128)S(1)} %fusion.356), channel_id=1, source_target_pairs={{16,0},{32,16},{48,32},{64,48},{80,64},{96,80},{112,96},{128,112},... | collective-permute-start | bytes 393224 | tf_op jit(solution)/shard_map/while/body/eval_jaxpr/ppermute | solution.py:17
  608.7 8.4 %collective-permute-start.1 = (f32[1,2,128,128]{3,2,1,0:T(8,128)S(1)}, f32[1,2,128,128]{3,2,1,0:T(8,128)S(1)}, u32[]{:S(2)}, u32[]{:S(2)}) collective-permute-start(f32[1,2,128,128]{3,2,1,0:T(8,128)S(1)} %fusion.356), channel_id=1, source_target_pairs={{16,0},{32,16},{48,32},{64,48},{80,64},{96,80},{112,96},{128,112},... | collective-permute-start | bytes 393224 | tf_op jit(solution)/shard_map/while/body/eval_jaxpr/ppermute | solution.py:17
  617.3 8.4 %collective-permute-start.1 = (f32[1,2,128,128]{3,2,1,0:T(8,128)S(1)}, f32[1,2,128,128]{3,2,1,0:T(8,128)S(1)}, u32[]{:S(2)}, u32[]{:S(2)}) collective-permute-start(f32[1,2,128,128]{3,2,1,0:T(8,128)S(1)} %fusion.356), channel_id=1, source_target_pairs={{16,0},{32,16},{48,32},{64,48},{80,64},{96,80},{112,96},{128,112},... | collective-permute-start | bytes 393224 | tf_op jit(solution)/shard_map/while/body/eval_jaxpr/ppermute | solution.py:17
  626.0 8.4 %collective-permute-start.1 = (f32[1,2,128,128]{3,2,1,0:T(8,128)S(1)}, f32[1,2,128,128]{3,2,1,0:T(8,128)S(1)}, u32[]{:S(2)}, u32[]{:S(2)}) collective-permute-start(f32[1,2,128,128]{3,2,1,0:T(8,128)S(1)} %fusion.356), channel_id=1, source_target_pairs={{16,0},{32,16},{48,32},{64,48},{80,64},{96,80},{112,96},{128,112},... | collective-permute-start | bytes 393224 | tf_op jit(solution)/shard_map/while/body/eval_jaxpr/ppermute | solution.py:17
  (21 other events, 546.9 us)
Sparse Core Ops, SparseCore 0:
  636.5 123.7 reduce-scatter.1
